TPU v7x, 256 devices: a whole 4x4x8 slice. The times are simulated.
256 devices in a mesh: lat: 8 (over z), lon: 16 (over x, y), mem: 2 (over core).
Axes of the slice: x: 4, y: 4, z: 8, core: 2. Of those that a mesh axis runs over, the one named last changes fastest.
Arguments:
- measured_inputs: bfloat16 [4096, 128, 256], P(('lat', 'lon', 'mem')), may hold values from -6 to 6
- target_sector: int32 [4096], P(('lat', 'lon', 'mem')), may hold values from 0 to 15, as said below
- hidden_member_fields: bfloat16 [2, 64, 128, 768], P('mem', 'lat', 'lon'), may hold values from -6 to 6
- analysis_adjoint: bfloat16 [2, 64, 128, 768], P('mem', 'lat', 'lon'), may hold values from -0.29882812 to 0.29882812
- inner_perceptron_coeffs: bfloat16 [256, 256], replicated, may hold values from -0.375 to 0.375
- outer_perceptron_coeffs: bfloat16 [256, 768], replicated, may hold values from -0.375 to 0.375
- probe_projector: bfloat16 [768, 768], replicated, may hold values from -0.21875 to 0.21875
- logit_sharpness: float32 [12], replicated, may hold values from 0.5 to 2.5
- adjacent_channel_coeffs: float32 [8, 768], replicated, may hold values from -0.7 to 0.7
Outputs:
- analysis: bfloat16 [2, 64, 128, 768], P('mem', 'lat', 'lon')
- in_weight_grad: float32 [256, 256], replicated
- out_weight_grad: float32 [256, 768], replicated
Inputs may be any that keep to these rules, and one draw needn't show every extreme that they name: `target_sector`: of the 16 blocks of one device at most 2 have one destination, and one destination has exactly 2; in every band and member one sector receives exactly 2 blocks from every device of the band, 32 in all, and no sector receives more.
All inputs are finite; a program needn't handle non-finite values.
Results may differ from a plain program's by a relative error of at most 0.012.
The roundings to bfloat16 on the way count: a program that leaves them out, or rounds other values in their place, can miss the bound.
Values may be sent and summed in bfloat16 or wider, within the bound.
No kernel may reach another device: no remote copies, remote signals or barrier semaphores. Data moves between devices by JAX's collectives and lax.ppermute only.
A program may use at most 192 MiB of HBM per device.

v0:
```python
import math

import jax
import jax.numpy as jnp
from jax import lax
from jax.experimental import pallas as pl
from jax.experimental.pallas import tpu as pltpu
from jax.sharding import PartitionSpec as P


CHANNELS_PER_ATT = 64
GROUPS = 3
LANES = 256
CHUNK_BLOCKS = 8
PIECE_BLOCKS = 8
MARK = 512.0
TABLE_ROWS = 5 * GROUPS * LANES
ROOM = 40


NEIGHBOURS = ((-1, -1), (-1, 0), (-1, 1), (0, -1), (0, 1), (1, -1), (1, 0), (1, 1))


def extended(block, sides, width):
    for axis, dim in sides:
        count = lax.axis_size(axis)
        forward = [(i, i + 1) for i in range(count - 1)]
        forward.append((count - 1, 0))
        backward = [(target, source) for source, target in forward]
        low = lax.ppermute(
            lax.slice_in_dim(block, block.shape[dim] - width, None, axis=dim), axis, forward
        )
        high = lax.ppermute(lax.slice_in_dim(block, 0, width, axis=dim), axis, backward)
        block = jnp.concatenate([low, block, high], axis=dim)
    return block


def mix_local(padded, keep_rows, adjacent_channel_coeffs, direction):
    values = padded.astype(jnp.float32) * keep_rows
    n_rows = padded.shape[0] - 2
    n_cols = padded.shape[1] - 2
    total = values[1 : 1 + n_rows, 1 : 1 + n_cols]
    for offset_idx, (row_step, col_step) in enumerate(NEIGHBOURS):
        row_start = 1 + direction * row_step
        col_start = 1 + direction * col_step
        total = (
            total
            + adjacent_channel_coeffs[offset_idx]
            * values[row_start : row_start + n_rows, col_start : col_start + n_cols]
        )
    return total


def pack_kernel(target_ref, blocks_ref, send_ref, count_ref, stage_ref, mark_ref, in_sem, out_sem, mark_sem):
    n_blocks = blocks_ref.shape[0]
    n_dest = send_ref.shape[0]
    cap = send_ref.shape[1]
    loads = [pltpu.make_async_copy(blocks_ref.at[b], stage_ref.at[b], in_sem.at[b]) for b in range(n_blocks)]
    for load in loads:
        load.start()
    mark_ref[...] = jnp.full(mark_ref.shape, MARK, mark_ref.dtype)
    for d in range(n_dest):
        count_ref[d] = 0

    def copy_of(b, dest, slot):
        return pltpu.make_async_copy(stage_ref.at[b], send_ref.at[dest, slot], out_sem.at[b])

    for b in range(n_blocks):
        dest = target_ref[b]
        slot = count_ref[dest]
        count_ref[dest] = slot + 1
        loads[b].wait()
        copy_of(b, dest, slot).start()

    def mark_of(d, slot):
        return pltpu.make_async_copy(
            mark_ref, send_ref.at[d, slot, pl.ds(0, mark_ref.shape[0])], mark_sem.at[d * cap + slot]
        )

    for d in range(n_dest):
        for slot in range(cap):

            @pl.when(count_ref[d] <= slot)
            def _():
                mark_of(d, slot).start()

    for b in range(n_blocks):
        copy_of(b, 0, 0).wait()
    for d in range(n_dest):
        for slot in range(cap):

            @pl.when(count_ref[d] <= slot)
            def _():
                mark_of(d, slot).wait()


def pack_blocks(target_sector, blocks, n_dest, cap):
    n_blocks, block_len, width = blocks.shape
    return pl.pallas_call(
        pack_kernel,
        out_shape=jax.ShapeDtypeStruct((n_dest, cap, block_len, width), blocks.dtype),
        in_specs=[
            pl.BlockSpec(memory_space=pltpu.SMEM),
            pl.BlockSpec(memory_space=pl.ANY),
        ],
        out_specs=pl.BlockSpec(memory_space=pl.ANY),
        scratch_shapes=[
            pltpu.SMEM((n_dest,), jnp.int32),
            pltpu.VMEM(blocks.shape, blocks.dtype),
            pltpu.VMEM((16, width), blocks.dtype),
            pltpu.SemaphoreType.DMA((n_blocks,)),
            pltpu.SemaphoreType.DMA((n_blocks,)),
            pltpu.SemaphoreType.DMA((n_dest * cap,)),
        ],
        name="pack_blocks",
    )(target_sector, blocks)


def block_mask():
    rows = lax.broadcasted_iota(jnp.int32, (LANES, LANES), 0) // CHANNELS_PER_ATT
    cols = lax.broadcasted_iota(jnp.int32, (LANES, LANES), 1) // CHANNELS_PER_ATT
    return rows == cols


def spread(values, group, mask):
    part = values[:, group * LANES : (group + 1) * LANES].astype(jnp.float32)
    return jnp.where(mask, jnp.concatenate([part] * (LANES // CHANNELS_PER_ATT), axis=0), 0.0)


def table_rows(kind, j):
    start = {"q": 0, "g": GROUPS, "gq": 2 * GROUPS, "o": 4 * GROUPS}[kind] + (2 * j if kind == "gq" else j)
    return slice(start * LANES, (start + (2 if kind == "gq" else 1)) * LANES)


def cells_kernel(cells_ref, grad_ref, probe_ref, outer_ref, table_hbm, xt_ref, self_ref, table_ref, sem):
    mask = block_mask()
    query = jnp.dot(cells_ref[...], probe_ref[...], preferred_element_type=jnp.float32)
    query = query.astype(jnp.bfloat16).astype(jnp.float32)
    cells = cells_ref[...].astype(jnp.float32)
    grad = grad_ref[...].astype(jnp.float32)
    for j in range(GROUPS):
        q_rows = spread(query, j, mask)
        g_rows = spread(grad, j, mask)
        table_ref[table_rows("gq", j), :] = jnp.concatenate([g_rows, q_rows], axis=0).astype(jnp.bfloat16)
        q_cols = q_rows.T
        g_cols = g_rows.T
        x_cols = spread(cells, j, mask).T
        table_ref[table_rows("q", j), :] = q_cols.astype(jnp.bfloat16)
        table_ref[table_rows("g", j), :] = g_cols.astype(jnp.bfloat16)
        xt_ref[j] = x_cols
        self_ref[0:1, j * LANES : (j + 1) * LANES] = jnp.sum(q_cols * x_cols, axis=0, keepdims=True)
        self_ref[1:2, j * LANES : (j + 1) * LANES] = jnp.sum(g_cols * x_cols, axis=0, keepdims=True)
        table_ref[table_rows("o", j), :] = (
            outer_ref[:, j * LANES : (j + 1) * LANES].astype(jnp.float32).T.astype(jnp.bfloat16)
        )
    copy = pltpu.make_async_copy(table_ref, table_hbm.at[pl.ds(0, table_ref.shape[0])], sem)
    copy.start()
    copy.wait()


def prepare_cells(cells, grad, probe, outer):
    width = cells.shape[1]
    hidden = outer.shape[0]
    vmem = pl.BlockSpec(memory_space=pltpu.VMEM)
    return pl.pallas_call(
        cells_kernel,
        out_shape=(
            jax.ShapeDtypeStruct((TABLE_ROWS * ROOM, hidden), jnp.bfloat16),
            jax.ShapeDtypeStruct((GROUPS, LANES, LANES), jnp.float32),
            jax.ShapeDtypeStruct((2, width), jnp.float32),
        ),
        out_specs=(pl.BlockSpec(memory_space=pl.ANY), vmem, vmem),
        scratch_shapes=[pltpu.VMEM((TABLE_ROWS, hidden), jnp.bfloat16), pltpu.SemaphoreType.DMA],
        compiler_params=pltpu.CompilerParams(vmem_limit_bytes=12 * 1024 * 1024),
        name="prepare_cells",
    )(cells, grad, probe, outer)


def contract_rows(left, right):
    return lax.dot_general(left, right, (((0,), (0,)), ((), ())), preferred_element_type=jnp.float32)


def tile_kernel(
    half_ref, recv_hbm, self_ref, norm_ref, inner_ref, outer_ref, table_hbm, xt_ref,
    state_ref, keep_ref, give_ref,
    recv_ref, head_ref, table_ref,
    x_s, f_s, p_s, d_s, h_s, m_s, l_s, peak_s, up_s, row_s, in_s, out_s, order_s, live_v, live_s, sem,
):
    n_slots, block_len, _ = recv_hbm.shape
    rows = CHUNK_BLOCKS * block_len
    f32 = jnp.float32
    bf16 = jnp.bfloat16

    head_copy = pltpu.make_async_copy(
        recv_hbm.at[:, pl.ds(0, head_ref.shape[1]), pl.ds(0, head_ref.shape[2])], head_ref, sem.at[1]
    )
    recv_copy = pltpu.make_async_copy(recv_hbm, recv_ref, sem.at[2])
    table_copy = pltpu.make_async_copy(table_hbm.at[pl.ds(0, TABLE_ROWS)], table_ref, sem.at[3])
    head_copy.start()
    recv_copy.start()
    table_copy.start()
    l_s[...] = jnp.ones_like(l_s)
    up_s[...] = jnp.zeros_like(up_s)
    in_s[...] = jnp.zeros_like(in_s)
    out_s[...] = jnp.zeros_like(out_s)
    head_copy.wait()
    for i in range(n_slots):
        head = head_ref[i].astype(f32)
        live_v[i : i + 1, :] = jnp.where(head[0:1, :] < MARK / 2, 1, 0)
    flags = pltpu.make_async_copy(live_v, live_s, sem.at[0])
    flags.start()
    flags.wait()
    count = jnp.int32(0)
    for i in range(n_slots):
        order_s[count] = i
        count = count + live_s[i, 0]
    recv_copy.wait()
    table_copy.wait()
    n_chunks = (count + CHUNK_BLOCKS - 1) // CHUNK_BLOCKS

    norm = norm_ref[...]
    self_score = self_ref[0:1, :] * norm
    m_s[...] = self_score

    def forward(k, carry):
        for i in range(CHUNK_BLOCKS):
            at = k * CHUNK_BLOCKS + i
            at_row = pl.ds(pl.multiple_of(at * block_len, block_len), block_len)

            @pl.when(at < count)
            def _():
                x_s[at_row, :] = recv_ref[order_s[at]]

            @pl.when(at >= count)
            def _():
                x_s[at_row, :] = jnp.zeros((block_len, x_s.shape[1]), bf16)

        start = pl.multiple_of(k * rows, rows)
        piece = PIECE_BLOCKS * block_len
        n_pieces = CHUNK_BLOCKS // PIECE_BLOCKS
        at = [pl.ds(start + i * piece, piece) for i in range(n_pieces)]
        columns = [slice(j * LANES, (j + 1) * LANES) for j in range(GROUPS)]
        bias = [jnp.where(k * CHUNK_BLOCKS + i < count, 0.0, -jnp.inf) for i in range(CHUNK_BLOCKS)]
        for i in range(n_pieces):
            pre = jnp.dot(x_s[at[i], :], inner_ref[...], preferred_element_type=f32)
            gate = 1.0 / (1.0 + jnp.exp(-pre))
            hidden = (pre * gate).astype(bf16)
            d_s[at[i], :] = gate * (1.0 + pre * (1.0 - gate))
            h_s[at[i], :] = hidden
            f_s[at[i], :] = jnp.dot(hidden, outer_ref[...], preferred_element_type=f32).astype(bf16)

        def score(j, i):
            raw = jnp.dot(f_s[at[i], columns[j]], table_ref[table_rows("q", j), :], preferred_element_type=f32)
            raw = raw * norm[:, columns[j]]
            top = None
            for n in range(PIECE_BLOCKS):
                part = raw[n * block_len : (n + 1) * block_len] + bias[i * PIECE_BLOCKS + n]
                p_s[pl.ds(start + i * piece + n * block_len, block_len), columns[j]] = part
                part_top = jnp.max(part, axis=0, keepdims=True)
                top = part_top if top is None else jnp.maximum(top, part_top)
            return top

        tops = [score(0, i) for i in range(n_pieces)]
        for j in range(GROUPS):
            cols = columns[j]
            old = m_s[:, cols]
            peak = old
            for top in tops:
                peak = jnp.maximum(peak, top)
            fade = jnp.exp(old - peak)
            total = l_s[:, cols] * fade
            update = up_s[j] * fade
            tops = []
            for i in range(n_pieces):
                terms = jnp.exp(p_s[at[i], cols] - peak)
                p_s[at[i], cols] = terms
                total = total + jnp.sum(terms, axis=0, keepdims=True)
                if j + 1 < GROUPS:
                    tops.append(score(j + 1, i))
                update = update + contract_rows(f_s[at[i], cols], terms.astype(bf16))
            m_s[:, cols] = peak
            peak_s[k, :, cols] = peak
            l_s[:, cols] = total
            up_s[j] = update
        return carry

    lax.fori_loop(0, n_chunks, forward, 0)

    mask = block_mask()
    inverse = 1.0 / l_s[...]
    peak = m_s[...]
    self_prob = jnp.exp(self_score - peak) * inverse
    self_weight = self_prob.astype(bf16).astype(f32)
    for j in range(GROUPS):
        cols = slice(j * LANES, (j + 1) * LANES)
        update = jnp.where(mask, up_s[j] * inverse[:, cols], 0.0)
        row_s[:, cols] = (
            jnp.sum(update * table_ref[table_rows("g", j), :].astype(f32), axis=0, keepdims=True)
            + self_prob[:, cols] * self_ref[1:2, cols]
        )
        x_cols = xt_ref[j]
        state = (x_cols + (update + self_weight[:, cols] * x_cols)).T
        total = state[0:CHANNELS_PER_ATT]
        for h in range(1, LANES // CHANNELS_PER_ATT):
            total = total + state[h * CHANNELS_PER_ATT : (h + 1) * CHANNELS_PER_ATT]
        state_ref[:, cols] = total.astype(bf16)

    row_total = row_s[...]

    def backward(k, carry):
        start = pl.multiple_of(k * rows, rows)
        here = pl.ds(start, rows)
        scale = jnp.exp(peak_s[k] - peak) * inverse
        scaled = scale * norm
        hidden = h_s[here, :]
        hidden_grad = jnp.zeros((rows, LANES), f32)
        for j in range(GROUPS):
            cols = slice(j * LANES, (j + 1) * LANES)
            terms = p_s[here, cols]
            weights = (terms * scale[:, cols]).astype(bf16)
            weight_grad = jnp.dot(
                f_s[here, cols], table_ref[table_rows("g", j), :], preferred_element_type=f32
            )
            logit_grad = ((terms * scaled[:, cols]) * (weight_grad - row_total[:, cols])).astype(bf16)
            feat_grad = jnp.dot(
                jnp.concatenate([weights, logit_grad], axis=1),
                table_ref[table_rows("gq", j), :],
                preferred_element_type=f32,
            ).astype(bf16)
            hidden_grad = hidden_grad + jnp.dot(
                feat_grad, table_ref[table_rows("o", j), :], preferred_element_type=f32
            )
            out_s[:, cols] = out_s[:, cols] + contract_rows(hidden, feat_grad)
        hidden_grad = (hidden_grad * d_s[here, :]).astype(bf16)
        in_s[...] = in_s[...] + contract_rows(x_s[here, :], hidden_grad)
        return carry

    lax.fori_loop(0, n_chunks, backward, 0)
    n_rows = keep_ref.shape[0]
    split = in_s.shape[1]
    for dst, half in ((keep_ref, half_ref[0]), (give_ref, 1 - half_ref[0])):
        here = pl.ds(pl.multiple_of(half * n_rows, n_rows), n_rows)
        dst[:, 0:split] = in_s[here, :].astype(bf16)
        dst[:, split:] = out_s[here, :].astype(bf16)


def tile_step(half, recv, table, xt, self_dots, norm, inner, outer, n_cells):
    n_slots, block_len, obs_width = recv.shape
    hidden, width = outer.shape
    n_tokens = n_slots * block_len
    n_chunks = n_slots // CHUNK_BLOCKS
    vmem = pl.BlockSpec(memory_space=pltpu.VMEM)
    return pl.pallas_call(
        tile_kernel,
        out_shape=(
            jax.ShapeDtypeStruct((n_cells, width), jnp.bfloat16),
            jax.ShapeDtypeStruct((obs_width // 2, hidden + width), jnp.bfloat16),
            jax.ShapeDtypeStruct((obs_width // 2, hidden + width), jnp.bfloat16),
        ),
        in_specs=[pl.BlockSpec(memory_space=pltpu.SMEM), pl.BlockSpec(memory_space=pl.ANY)]
        + [vmem] * 4
        + [pl.BlockSpec(memory_space=pl.ANY), vmem],
        out_specs=(vmem, vmem, vmem),
        scratch_shapes=[
            pltpu.VMEM(recv.shape, recv.dtype),
            pltpu.VMEM((n_slots, 16, 128), recv.dtype),
            pltpu.VMEM((TABLE_ROWS, hidden), table.dtype),
            pltpu.VMEM((n_tokens, obs_width), jnp.bfloat16),
            pltpu.VMEM((n_tokens, width), jnp.bfloat16),
            pltpu.VMEM((n_tokens, width), jnp.float32),
            pltpu.VMEM((n_tokens, hidden), jnp.float32),
            pltpu.VMEM((n_tokens, hidden), jnp.bfloat16),
            pltpu.VMEM((1, width), jnp.float32),
            pltpu.VMEM((1, width), jnp.float32),
            pltpu.VMEM((n_chunks, 1, width), jnp.float32),
            pltpu.VMEM((GROUPS, LANES, LANES), jnp.float32),
            pltpu.VMEM((1, width), jnp.float32),
            pltpu.VMEM((obs_width, hidden), jnp.float32),
            pltpu.VMEM((hidden, width), jnp.float32),
            pltpu.SMEM((n_slots + 1,), jnp.int32),
            pltpu.VMEM((n_slots, 128), jnp.int32),
            pltpu.SMEM((n_slots, 128), jnp.int32),
            pltpu.SemaphoreType.DMA((4,)),
        ],
        compiler_params=pltpu.CompilerParams(vmem_limit_bytes=44 * 1024 * 1024),
        name="tile_step",
    )(half, recv, self_dots, norm, inner, outer, table, xt)


def unfold_kernel(half_ref, own_ref, other_ref, in_ref, out_ref):
    rows, _ = own_ref.shape
    hidden = in_ref.shape[1]
    own_at = pl.ds(pl.multiple_of(half_ref[0] * rows, rows), rows)
    other_at = pl.ds(pl.multiple_of((1 - half_ref[0]) * rows, rows), rows)
    in_ref[own_at, :] = own_ref[:, 0:hidden].astype(jnp.float32)
    in_ref[other_at, :] = other_ref[:, 0:hidden].astype(jnp.float32)
    out_ref[own_at, :] = own_ref[:, hidden:].astype(jnp.float32)
    out_ref[other_at, :] = other_ref[:, hidden:].astype(jnp.float32)


def unfold(half, own, other, hidden):
    rows, cols = own.shape
    vmem = pl.BlockSpec(memory_space=pltpu.VMEM)
    return pl.pallas_call(
        unfold_kernel,
        out_shape=(
            jax.ShapeDtypeStruct((2 * rows, hidden), jnp.float32),
            jax.ShapeDtypeStruct((2 * rows, cols - hidden), jnp.float32),
        ),
        in_specs=[pl.BlockSpec(memory_space=pltpu.SMEM), vmem, vmem],
        out_specs=(vmem, vmem),
        compiler_params=pltpu.CompilerParams(vmem_limit_bytes=8 * 1024 * 1024),
        name="unfold",
    )(half, own, other)


def reduce_everywhere(half, keep, give, hidden):
    n_rows, n_cols = keep.shape
    lon_count = lax.axis_size("lon")
    lat_count = lax.axis_size("lat")
    swap = [(0, 1), (1, 0)]
    mine = keep.astype(jnp.float32)
    theirs = lax.ppermute(give, "mem", swap)
    pair = (mine + theirs.astype(jnp.float32)).astype(jnp.bfloat16)
    pieces = lax.all_to_all(
        pair.reshape(lon_count, n_rows // lon_count, n_cols), "lon", split_axis=0, concat_axis=0, tiled=True
    )
    part = jnp.sum(pieces.astype(jnp.float32), axis=0).astype(jnp.bfloat16)
    peers = lax.all_to_all(
        jnp.broadcast_to(part[None], (lat_count,) + part.shape), "lat", split_axis=0, concat_axis=0, tiled=True
    )
    total = jnp.sum(peers.astype(jnp.float32), axis=0).astype(jnp.bfloat16)
    own = lax.all_to_all(
        jnp.broadcast_to(total[None], (lon_count,) + total.shape), "lon", split_axis=0, concat_axis=0, tiled=True
    ).reshape(n_rows, n_cols)
    other = lax.ppermute(own, "mem", swap)
    return unfold(half, own, other, hidden)


def per_device(
    measured_inputs,
    target_sector,
    hidden_member_fields,
    analysis_adjoint,
    inner_perceptron_coeffs,
    outer_perceptron_coeffs,
    probe_projector,
    logit_sharpness,
    adjacent_channel_coeffs,
):
    lon_count = lax.axis_size("lon")
    lat_count = lax.axis_size("lat")
    block_count = target_sector.shape[0]
    model_width = hidden_member_fields.shape[3]
    hidden_width = inner_perceptron_coeffs.shape[1]
    cell_rows = hidden_member_fields.shape[1]
    cell_cols = hidden_member_fields.shape[2]
    n_cells = cell_rows * cell_cols
    cap_slots = max(2, 2 * block_count // lon_count)
    send_blocks = pack_blocks(target_sector, measured_inputs, lon_count, cap_slots)
    obs_blocks = lax.all_to_all(send_blocks, "lon", split_axis=0, concat_axis=0, tiled=True)
    cot_padded = extended(analysis_adjoint[0], (("lon", 1), ("lat", 0)), 1)
    lat_index = lax.axis_index("lat")
    row_ids = lax.broadcasted_iota(jnp.int32, (cell_rows + 2, 1, 1), 0)
    outside = ((row_ids == 0) & (lat_index == 0)) | (
        (row_ids == cell_rows + 1) & (lat_index == lat_count - 1)
    )
    keep_rows = jnp.where(outside, 0.0, 1.0)
    hidden_field_adjoint = (
        mix_local(cot_padded, keep_rows, adjacent_channel_coeffs, -1)
        .astype(jnp.bfloat16)
        .reshape(n_cells, model_width)
    )
    grid_point_entries = hidden_member_fields.reshape(n_cells, model_width)
    prepared = prepare_cells(
        grid_point_entries, hidden_field_adjoint, probe_projector, outer_perceptron_coeffs
    )
    table, xt, self_dots = prepared
    norm = jnp.repeat(logit_sharpness / math.sqrt(CHANNELS_PER_ATT), n_cells)[None, :]
    half = lax.axis_index("mem").astype(jnp.int32).reshape(1)
    revised_analysis, keep, give = tile_step(
        half, obs_blocks.reshape((-1,) + obs_blocks.shape[2:]), table, xt, self_dots, norm,
        inner_perceptron_coeffs, outer_perceptron_coeffs, n_cells,
    )
    in_grad, out_grad = reduce_everywhere(half, keep, give, hidden_width)
    state_grid = revised_analysis.reshape(cell_rows, cell_cols, model_width)
    state_padded = extended(state_grid, (("lon", 1), ("lat", 0)), 1)
    analysis = (
        mix_local(state_padded, keep_rows, adjacent_channel_coeffs, 1)
        .astype(jnp.bfloat16)
        .reshape(hidden_member_fields.shape)
    )
    return (analysis, in_grad, out_grad)


def solution(mesh):
    in_specs = (
        P(("lat", "lon", "mem"), None, None),
        P(("lat", "lon", "mem")),
        P("mem", "lat", "lon", None),
        P("mem", "lat", "lon", None),
        P(),
        P(),
        P(),
        P(),
        P(),
    )
    out_specs = (P("mem", "lat", "lon", None), P(), P())

    return jax.shard_map(per_device, mesh=mesh, in_specs=in_specs, out_specs=out_specs, check_vma=False)
```

profile of v0, /device:TPU:2, one launch (start us, length us, event | category | flops | bytes accessed | tf_op | source)
XLA Modules:
  0.0 118.2 jit_solution(16860831784090447875)
XLA Ops:
  0.6 3.2 %pack_blocks.1 = bf16[16,2,128,256]{3,2,1,0:T(8,128)(2,1)} custom-call(s32[16]{0:T(128)} %target_ref.1, bf16[16,128,256]{2,1,0:T(8,128)(2,1)} %blocks_ref.1), custom_call_target="tpu_custom_call" | custom-call | tf_op jit(solution)/shard_map/pack_blocks/pallas_call | solution.py:99
  3.9 7.6 %all-to-all-start = ((bf16[16,2,128,256]{3,2,1,0:T(8,128)(2,1)}), bf16[16,2,128,256]{3,2,1,0:T(8,128)(2,1)S(1)}, u32[]{:S(2)}, u32[]{:S(2)}) async-start(bf16[16,2,128,256]{3,2,1,0:T(8,128)(2,1)} %pack_blocks.1), calls=%async_computation | async-start | bytes 4194304 | tf_op jit(solution)/shard_map/all_to_all | solution.py:461
  11.6 1.5 %collective-permute-start = (bf16[8,1,768]{2,1,0:T(2,128)(2,1)S(1)}, bf16[8,1,768]{2,1,0:T(2,128)(2,1)S(1)}, u32[]{:S(2)}, u32[]{:S(2)}) collective-permute-start(bf16[8,1,768]{2,1,0:T(2,128)(2,1)S(1)} %get-tuple-element.33), channel_id=1, source_target_pairs={{0,2},{2,4},{4,6},{6,8},{8,10},{10,12},{12,14},{14,16},{16,18},{18... | collective-permute-start | bytes 36872 | tf_op jit(solution)/shard_map/ppermute | solution.py:30
  13.1 2.7 %collective-permute-start.1 = (bf16[8,1,768]{2,1,0:T(2,128)(2,1)S(1)}, bf16[8,1,768]{2,1,0:T(2,128)(2,1)S(1)}, u32[]{:S(2)}, u32[]{:S(2)}) collective-permute-start(bf16[8,1,768]{2,1,0:T(2,128)(2,1)S(1)} %get-tuple-element.34), channel_id=1, source_target_pairs={{2,0},{4,2},{6,4},{8,6},{10,8},{12,10},{14,12},{16,14},{18,16},{20... | collective-permute-start | bytes 36872 | tf_op jit(solution)/shard_map/ppermute | solution.py:33
  15.9 22.3 %collective-permute-done = bf16[8,1,768]{2,1,0:T(2,128)(2,1)S(1)} collective-permute-done((bf16[8,1,768]{2,1,0:T(2,128)(2,1)S(1)}, bf16[8,1,768]{2,1,0:T(2,128)(2,1)S(1)}, u32[]{:S(2)}, u32[]{:S(2)}) %collective-permute-start) | collective-permute-done | bytes 12320 | tf_op jit(solution)/shard_map/ppermute | solution.py:30
  38.2 2.0 %collective-permute-start.2 = (bf16[1,10,768]{2,1,0:T(8,128)(2,1)S(1)}, bf16[1,10,768]{2,1,0:T(8,128)(2,1)S(1)}, u32[]{:S(2)}, u32[]{:S(2)}) collective-permute-start(bf16[1,10,768]{2,1,0:T(8,128)(2,1)S(1)} %get-tuple-element.29), channel_id=1, source_target_pairs={{0,32},{32,64},{64,96},{96,128},{128,160},{160,192},{192,224},{224... | collective-permute-start | bytes 46088 | tf_op jit(solution)/shard_map/ppermute | solution.py:30
  40.3 3.9 %collective-permute-start.3 = (bf16[1,10,768]{2,1,0:T(8,128)(2,1)S(1)}, bf16[1,10,768]{2,1,0:T(8,128)(2,1)S(1)}, u32[]{:S(2)}, u32[]{:S(2)}) collective-permute-start(bf16[1,10,768]{2,1,0:T(8,128)(2,1)S(1)} %get-tuple-element.30), channel_id=1, source_target_pairs={{32,0},{64,32},{96,64},{128,96},{160,128},{192,160},{224,192},{0,2... | collective-permute-start | bytes 46088 | tf_op jit(solution)/shard_map/ppermute | solution.py:33
  44.4 1.6 %collective-permute-done.2 = bf16[1,10,768]{2,1,0:T(8,128)(2,1)S(1)} collective-permute-done((bf16[1,10,768]{2,1,0:T(8,128)(2,1)S(1)}, bf16[1,10,768]{2,1,0:T(8,128)(2,1)S(1)}, u32[]{:S(2)}, u32[]{:S(2)}) %collective-permute-start.2) | collective-permute-done | bytes 15392 | tf_op jit(solution)/shard_map/ppermute | solution.py:30
  46.1 0.2 fusion.19.grad_ref
  46.2 2.0 %prepare_cells.1 = (bf16[153600,256]{1,0:T(8,128)(2,1)}, f32[3,256,256]{2,1,0:T(8,128)S(1)}, f32[2,768]{1,0:T(2,128)S(1)}) custom-call(bf16[64,768]{1,0:T(8,128)(2,1)S(1)} %bitcast.18, bf16[64,768]{1,0:T(8,128)(2,1)S(1)} %fusion.19.grad_ref, bf16[768,768]{1,0:T(8,128)(2,1)S(1)} %copy-done.1, bf16[256,768]{1,0:T(8,128)(2,1)S(1)} %copy-done), custom_call_target="tpu_custom_call" | custom-call | tf_op jit(solution)/shard_map/prepare_cells/pallas_call | solution.py:165
  48.3 11.8 %tile_step.1 = (bf16[64,768]{1,0:T(8,128)(2,1)S(1)}, bf16[128,1024]{1,0:T(8,128)(2,1)S(1)}, bf16[128,1024]{1,0:T(8,128)(2,1)S(1)}) custom-call(s32[1]{0:T(128)} %bitcast.half_ref, bf16[32,128,256]{2,1,0:T(8,128)(2,1)S(1)} %bitcast.12, f32[2,768]{1,0:T(2,128)S(1)} %get-tuple-element.11.self_ref, f32[1,768]{1,0:T(1,128)S(1)} %broadcast_in_dim_reshape.3.norm_ref, ...), custom_call_target="tpu_custom_call" | custom-call | tf_op jit(solution)/shard_map/tile_step/pallas_call | solution.py:353
  60.2 1.5 %collective-permute-done.8 = bf16[128,1024]{1,0:T(8,128)(2,1)S(1)} collective-permute-done((bf16[128,1024]{1,0:T(8,128)(2,1)S(1)}, bf16[128,1024]{1,0:T(8,128)(2,1)S(1)}, u32[]{:S(2)}, u32[]{:S(2)}) %collective-permute-start.8) | collective-permute-done | bytes 262176 | tf_op jit(solution)/shard_map/ppermute | solution.py:423
  61.8 22.1 %all_to_all.20 = bf16[16,8,1024]{2,1,0:T(8,128)(2,1)S(1)} all-to-all(bf16[16,8,1024]{2,1,0:T(8,128)(2,1)S(1)} %fusion), channel_id=1, replica_groups=mesh['lat'=8,'lon'=16,'mem'=2] {'lon'}, dimensions={0} | all-to-all | bytes 524288 | tf_op jit(solution)/shard_map/all_to_all | solution.py:425
  83.9 14.7 %all_to_all.21 = bf16[8,8,1024]{2,1,0:T(8,128)(2,1)S(1)} all-to-all(bf16[8,8,1024]{2,1,0:T(8,128)(2,1)S(1)} %broadcast_in_dim.26), channel_id=1, replica_groups=mesh['lat'=8,'lon'=16,'mem'=2] {'lat'}, dimensions={0} | all-to-all | bytes 262144 | tf_op jit(solution)/shard_map/all_to_all | solution.py:429
  98.6 0.7 broadcast_in_dim.27
  99.3 5.3 %all-to-all-start.3 = ((bf16[16,8,1024]{2,1,0:T(8,128)(2,1)}), bf16[16,8,1024]{2,1,0:T(8,128)(2,1)S(1)}, u32[]{:S(2)}, u32[]{:S(2)}) async-start(bf16[16,8,1024]{2,1,0:T(8,128)(2,1)} %broadcast_in_dim.27), calls=%async_computation.3 | async-start | bytes 524288 | tf_op jit(solution)/shard_map/all_to_all | solution.py:433
  104.7 1.7 %collective-permute-start.4 = (bf16[8,1,768]{2,1,0:T(2,128)(2,1)S(1)}, bf16[8,1,768]{2,1,0:T(2,128)(2,1)S(1)}, u32[]{:S(2)}, u32[]{:S(2)}) collective-permute-start(bf16[8,1,768]{2,1,0:T(2,128)(2,1)S(1)} %get-tuple-element.31), channel_id=1, source_target_pairs={{0,2},{2,4},{4,6},{6,8},{8,10},{10,12},{12,14},{14,16},{16,18},{18... | collective-permute-start | bytes 36872 | tf_op jit(solution)/shard_map/ppermute | solution.py:30
  106.4 2.7 %collective-permute-start.5 = (bf16[8,1,768]{2,1,0:T(2,128)(2,1)S(1)}, bf16[8,1,768]{2,1,0:T(2,128)(2,1)S(1)}, u32[]{:S(2)}, u32[]{:S(2)}) collective-permute-start(bf16[8,1,768]{2,1,0:T(2,128)(2,1)S(1)} %get-tuple-element.32), channel_id=1, source_target_pairs={{2,0},{4,2},{6,4},{8,6},{10,8},{12,10},{14,12},{16,14},{18,16},{20... | collective-permute-start | bytes 36872 | tf_op jit(solution)/shard_map/ppermute | solution.py:33
  109.1 2.0 %collective-permute-done.4 = bf16[8,1,768]{2,1,0:T(2,128)(2,1)S(1)} collective-permute-done((bf16[8,1,768]{2,1,0:T(2,128)(2,1)S(1)}, bf16[8,1,768]{2,1,0:T(2,128)(2,1)S(1)}, u32[]{:S(2)}, u32[]{:S(2)}) %collective-permute-start.4) | collective-permute-done | bytes 12320 | tf_op jit(solution)/shard_map/ppermute | solution.py:30
  111.1 0.6 collective-permute-start.6
  111.8 2.7 %collective-permute-start.7 = (bf16[1,10,768]{2,1,0:T(8,128)(2,1)S(1)}, bf16[1,10,768]{2,1,0:T(8,128)(2,1)S(1)}, u32[]{:S(2)}, u32[]{:S(2)}) collective-permute-start(bf16[1,10,768]{2,1,0:T(8,128)(2,1)S(1)} %get-tuple-element.28), channel_id=1, source_target_pairs={{32,0},{64,32},{96,64},{128,96},{160,128},{192,160},{224,192},{0,2... | collective-permute-start | bytes 46088 | tf_op jit(solution)/shard_map/ppermute | solution.py:33
  114.4 1.8 %collective-permute-done.6 = bf16[1,10,768]{2,1,0:T(8,128)(2,1)S(1)} collective-permute-done((bf16[1,10,768]{2,1,0:T(8,128)(2,1)S(1)}, bf16[1,10,768]{2,1,0:T(8,128)(2,1)S(1)}, u32[]{:S(2)}, u32[]{:S(2)}) %collective-permute-start.6) | collective-permute-done | bytes 15392 | tf_op jit(solution)/shard_map/ppermute | solution.py:30
  116.4 0.8 fusion.20
  117.2 1.0 unfold.1
  (38 shorter events, 0.9 us)
Async XLA Ops:
  3.9 7.6 %copy-start.4 = (bf16[1,8,8,768]{3,2,1,0:T(8,128)(2,1)S(1)}, bf16[1,8,8,768]{3,2,1,0:T(8,128)(2,1)}, u32[]{:S(2)}) copy-start(bf16[1,8,8,768]{3,2,1,0:T(8,128)(2,1)} %param.12) | copy-start | bytes 294916
  3.9 11.9 %copy-start.6 = (f32[12]{0:T(128)S(1)}, f32[12]{0:T(128)}, u32[]{:S(2)}) copy-start(f32[12]{0:T(128)} %param.16) | copy-start | bytes 148
  3.9 11.9 %copy-start.5 = (f32[8,768]{1,0:T(8,128)S(1)}, f32[8,768]{1,0:T(8,128)}, u32[]{:S(2)}) copy-start(f32[8,768]{1,0:T(8,128)} %param.17) | copy-start | bytes 73732
  3.9 44.3 %all-to-all-start = ((bf16[16,2,128,256]{3,2,1,0:T(8,128)(2,1)}), bf16[16,2,128,256]{3,2,1,0:T(8,128)(2,1)S(1)}, u32[]{:S(2)}, u32[]{:S(2)}) async-start(bf16[16,2,128,256]{3,2,1,0:T(8,128)(2,1)} %pack_blocks.1), calls=%async_computation | async-start | bytes 4194304 | tf_op jit(solution)/shard_map/all_to_all | solution.py:461
  11.5 34.7 %copy-start = (bf16[256,768]{1,0:T(8,128)(2,1)S(1)}, bf16[256,768]{1,0:T(8,128)(2,1)}, u32[]{:S(2)}) copy-start(bf16[256,768]{1,0:T(8,128)(2,1)} %outer_ref.3) | copy-start | bytes 1179652
  11.5 34.7 %copy-start.3 = (bf16[1,8,8,768]{3,2,1,0:T(8,128)(2,1)S(1)}, bf16[1,8,8,768]{3,2,1,0:T(8,128)(2,1)}, u32[]{:S(2)}) copy-start(bf16[1,8,8,768]{3,2,1,0:T(8,128)(2,1)} %param.11) | copy-start | bytes 294916
  11.6 26.6 %collective-permute-start = (bf16[8,1,768]{2,1,0:T(2,128)(2,1)S(1)}, bf16[8,1,768]{2,1,0:T(2,128)(2,1)S(1)}, u32[]{:S(2)}, u32[]{:S(2)}) collective-permute-start(bf16[8,1,768]{2,1,0:T(2,128)(2,1)S(1)} %get-tuple-element.33), channel_id=1, source_target_pairs={{0,2},{2,4},{4,6},{6,8},{8,10},{10,12},{12,14},{14,16},{16,18},{18... | collective-permute-start | bytes 36872 | tf_op jit(solution)/shard_map/ppermute | solution.py:30
  13.1 25.1 %collective-permute-start.1 = (bf16[8,1,768]{2,1,0:T(2,128)(2,1)S(1)}, bf16[8,1,768]{2,1,0:T(2,128)(2,1)S(1)}, u32[]{:S(2)}, u32[]{:S(2)}) collective-permute-start(bf16[8,1,768]{2,1,0:T(2,128)(2,1)S(1)} %get-tuple-element.34), channel_id=1, source_target_pairs={{2,0},{4,2},{6,4},{8,6},{10,8},{12,10},{14,12},{16,14},{18,16},{20... | collective-permute-start | bytes 36872 | tf_op jit(solution)/shard_map/ppermute | solution.py:33
  38.2 7.7 %collective-permute-start.2 = (bf16[1,10,768]{2,1,0:T(8,128)(2,1)S(1)}, bf16[1,10,768]{2,1,0:T(8,128)(2,1)S(1)}, u32[]{:S(2)}, u32[]{:S(2)}) collective-permute-start(bf16[1,10,768]{2,1,0:T(8,128)(2,1)S(1)} %get-tuple-element.29), channel_id=1, source_target_pairs={{0,32},{32,64},{64,96},{96,128},{128,160},{160,192},{192,224},{224... | collective-permute-start | bytes 46088 | tf_op jit(solution)/shard_map/ppermute | solution.py:30
  40.3 5.6 %collective-permute-start.3 = (bf16[1,10,768]{2,1,0:T(8,128)(2,1)S(1)}, bf16[1,10,768]{2,1,0:T(8,128)(2,1)S(1)}, u32[]{:S(2)}, u32[]{:S(2)}) collective-permute-start(bf16[1,10,768]{2,1,0:T(8,128)(2,1)S(1)} %get-tuple-element.30), channel_id=1, source_target_pairs={{32,0},{64,32},{96,64},{128,96},{160,128},{192,160},{224,192},{0,2... | collective-permute-start | bytes 46088 | tf_op jit(solution)/shard_map/ppermute | solution.py:33
  44.4 1.9 %copy-start.1 = (bf16[768,768]{1,0:T(8,128)(2,1)S(1)}, bf16[768,768]{1,0:T(8,128)(2,1)}, u32[]{:S(2)}) copy-start(bf16[768,768]{1,0:T(8,128)(2,1)} %probe_ref.1) | copy-start | bytes 3538948
  44.4 3.9 %copy-start.2 = (bf16[256,256]{1,0:T(8,128)(2,1)S(1)}, bf16[256,256]{1,0:T(8,128)(2,1)}, u32[]{:S(2)}) copy-start(bf16[256,256]{1,0:T(8,128)(2,1)} %inner_ref.1) | copy-start | bytes 393220
  60.1 1.6 %collective-permute-start.8 = (bf16[128,1024]{1,0:T(8,128)(2,1)S(1)}, bf16[128,1024]{1,0:T(8,128)(2,1)S(1)}, u32[]{:S(2)}, u32[]{:S(2)}) collective-permute-start(bf16[128,1024]{1,0:T(8,128)(2,1)S(1)} %get-tuple-element.16), channel_id=1, source_target_pairs={{0,1},{1,0},{2,3},{3,2},{4,5},{5,4},{6,7},{7,6},{8,9},{9,8},{10,11... | collective-permute-start | bytes 786440 | tf_op jit(solution)/shard_map/ppermute | solution.py:423
  99.3 15.1 %all-to-all-start.3 = ((bf16[16,8,1024]{2,1,0:T(8,128)(2,1)}), bf16[16,8,1024]{2,1,0:T(8,128)(2,1)S(1)}, u32[]{:S(2)}, u32[]{:S(2)}) async-start(bf16[16,8,1024]{2,1,0:T(8,128)(2,1)} %broadcast_in_dim.27), calls=%async_computation.3 | async-start | bytes 524288 | tf_op jit(solution)/shard_map/all_to_all | solution.py:433
  104.7 6.4 %collective-permute-start.4 = (bf16[8,1,768]{2,1,0:T(2,128)(2,1)S(1)}, bf16[8,1,768]{2,1,0:T(2,128)(2,1)S(1)}, u32[]{:S(2)}, u32[]{:S(2)}) collective-permute-start(bf16[8,1,768]{2,1,0:T(2,128)(2,1)S(1)} %get-tuple-element.31), channel_id=1, source_target_pairs={{0,2},{2,4},{4,6},{6,8},{8,10},{10,12},{12,14},{14,16},{16,18},{18... | collective-permute-start | bytes 36872 | tf_op jit(solution)/shard_map/ppermute | solution.py:30
  106.4 4.7 %collective-permute-start.5 = (bf16[8,1,768]{2,1,0:T(2,128)(2,1)S(1)}, bf16[8,1,768]{2,1,0:T(2,128)(2,1)S(1)}, u32[]{:S(2)}, u32[]{:S(2)}) collective-permute-start(bf16[8,1,768]{2,1,0:T(2,128)(2,1)S(1)} %get-tuple-element.32), channel_id=1, source_target_pairs={{2,0},{4,2},{6,4},{8,6},{10,8},{12,10},{14,12},{16,14},{18,16},{20... | collective-permute-start | bytes 36872 | tf_op jit(solution)/shard_map/ppermute | solution.py:33
  111.1 5.1 %collective-permute-start.6 = (bf16[1,10,768]{2,1,0:T(8,128)(2,1)S(1)}, bf16[1,10,768]{2,1,0:T(8,128)(2,1)S(1)}, u32[]{:S(2)}, u32[]{:S(2)}) collective-permute-start(bf16[1,10,768]{2,1,0:T(8,128)(2,1)S(1)} %get-tuple-element.27), channel_id=1, source_target_pairs={{0,32},{32,64},{64,96},{96,128},{128,160},{160,192},{192,224},{224... | collective-permute-start | bytes 46088 | tf_op jit(solution)/shard_map/ppermute | solution.py:30
  111.8 4.5 %collective-permute-start.7 = (bf16[1,10,768]{2,1,0:T(8,128)(2,1)S(1)}, bf16[1,10,768]{2,1,0:T(8,128)(2,1)S(1)}, u32[]{:S(2)}, u32[]{:S(2)}) collective-permute-start(bf16[1,10,768]{2,1,0:T(8,128)(2,1)S(1)} %get-tuple-element.28), channel_id=1, source_target_pairs={{32,0},{64,32},{96,64},{128,96},{160,128},{192,160},{224,192},{0,2... | collective-permute-start | bytes 46088 | tf_op jit(solution)/shard_map/ppermute | solution.py:33
  114.4 2.7 %collective-permute-start.9 = (bf16[128,1024]{1,0:T(8,128)(2,1)S(1)}, bf16[128,1024]{1,0:T(8,128)(2,1)S(1)}, u32[]{:S(2)}, u32[]{:S(2)}) collective-permute-start(bf16[128,1024]{1,0:T(8,128)(2,1)S(1)} %bitcast.13), channel_id=1, source_target_pairs={{0,1},{1,0},{2,3},{3,2},{4,5},{5,4},{6,7},{7,6},{8,9},{9,8},{10,11... | collective-permute-start | bytes 786440 | tf_op jit(solution)/shard_map/ppermute | solution.py:436
where the time goes:
time: 120 us; the launch traced here: 118 us
  blocking collectives  36.8 us (31%)
  starting transfers between devices  30.9 us (26%)
  waiting for transfers between devices  29.2 us (24%)
  Pallas kernels  18 us (15%)
  other arithmetic  1.37 us (1%)
    ppermute x4, waiting for transfers between devices, extended(): lax.ppermute(lax.slice_in_dim(block, block.shape[dim] - width, None, axis...  27.7 us
    all_to_all x1, blocking collectives, reduce_everywhere(): lax.all_to_all(pair.reshape(lon_count, n_rows // lon_count, n_cols), 'lon...  22.1 us
    all_to_all x1, blocking collectives, reduce_everywhere(): lax.all_to_all(jnp.broadcast_to(part[None], (lat_count,) + part.shape), '...  14.7 us
    ppermute x4, starting transfers between devices, extended(): lax.ppermute(lax.slice_in_dim(block, 0, width, axis=dim), axis, backward)  11.9 us
    pallas_call x1, Pallas kernels, tile_step(): pl.pallas_call(tile_kernel, out_shape=(jax.ShapeDtypeStruct((n_cells, wid...  11.8 us
    all_to_all x1, starting transfers between devices, per_device(): lax.all_to_all(send_blocks, 'lon', split_axis=0, concat_axis=0, tiled=True)  7.59 us
    ppermute x4, starting transfers between devices, extended(): lax.ppermute(lax.slice_in_dim(block, block.shape[dim] - width, None, axis...  5.95 us
    all_to_all x1, starting transfers between devices, reduce_everywhere(): lax.all_to_all(jnp.broadcast_to(total[None], (lon_count,) + total.shape),...  5.35 us
  transfers between devices with their start and end apart: 12, of which 5 were waited for; matrix products, arithmetic and copies ran while one was open for 1% of the time, Pallas kernels for 2%

commit v1 on v0

--- a/solution.py
+++ b/solution.py
@@ -21,12 +21,17 @@
 NEIGHBOURS = ((-1, -1), (-1, 0), (-1, 1), (0, -1), (0, 1), (1, -1), (1, 0), (1, 1))
 
 
-def extended(block, sides, width):
+def extended(block, sides, width, edges=None):
     for axis, dim in sides:
         count = lax.axis_size(axis)
         forward = [(i, i + 1) for i in range(count - 1)]
         forward.append((count - 1, 0))
         backward = [(target, source) for source, target in forward]
+        if edges is not None and dim == 1:
+            low = lax.ppermute(edges[1], axis, forward)[:, None]
+            high = lax.ppermute(edges[0], axis, backward)[:, None]
+            block = jnp.concatenate([low, block, high], axis=dim)
+            continue
         low = lax.ppermute(
             lax.slice_in_dim(block, block.shape[dim] - width, None, axis=dim), axis, forward
         )
@@ -51,11 +56,16 @@
     return total
 
 
-def pack_kernel(target_ref, blocks_ref, send_ref, count_ref, stage_ref, mark_ref, in_sem, out_sem, mark_sem):
+def pack_kernel(
+    target_ref, blocks_ref, field_ref, send_ref, first_ref, last_ref,
+    count_ref, stage_ref, cells_ref, mark_ref, in_sem, out_sem, mark_sem, cell_sem,
+):
     n_blocks = blocks_ref.shape[0]
     n_dest = send_ref.shape[0]
     cap = send_ref.shape[1]
     loads = [pltpu.make_async_copy(blocks_ref.at[b], stage_ref.at[b], in_sem.at[b]) for b in range(n_blocks)]
+    cells = pltpu.make_async_copy(field_ref, cells_ref, cell_sem)
+    cells.start()
     for load in loads:
         load.start()
     mark_ref[...] = jnp.full(mark_ref.shape, MARK, mark_ref.dtype)
@@ -84,6 +94,10 @@
             def _():
                 mark_of(d, slot).start()
 
+    cells.wait()
+    grid = [cells_ref[row].astype(jnp.float32) for row in range(cells_ref.shape[0])]
+    first_ref[...] = jnp.concatenate([row[0:1] for row in grid], axis=0).astype(first_ref.dtype)
+    last_ref[...] = jnp.concatenate([row[-1:] for row in grid], axis=0).astype(last_ref.dtype)
     for b in range(n_blocks):
         copy_of(b, 0, 0).wait()
     for d in range(n_dest):
@@ -94,26 +108,34 @@
                 mark_of(d, slot).wait()
 
 
-def pack_blocks(target_sector, blocks, n_dest, cap):
+def pack_blocks(target_sector, blocks, field, n_dest, cap):
     n_blocks, block_len, width = blocks.shape
+    vmem = pl.BlockSpec(memory_space=pltpu.VMEM)
     return pl.pallas_call(
         pack_kernel,
-        out_shape=jax.ShapeDtypeStruct((n_dest, cap, block_len, width), blocks.dtype),
+        out_shape=(
+            jax.ShapeDtypeStruct((n_dest, cap, block_len, width), blocks.dtype),
+            jax.ShapeDtypeStruct((field.shape[0], field.shape[2]), field.dtype),
+            jax.ShapeDtypeStruct((field.shape[0], field.shape[2]), field.dtype),
+        ),
         in_specs=[
             pl.BlockSpec(memory_space=pltpu.SMEM),
             pl.BlockSpec(memory_space=pl.ANY),
+            pl.BlockSpec(memory_space=pl.ANY),
         ],
-        out_specs=pl.BlockSpec(memory_space=pl.ANY),
+        out_specs=(pl.BlockSpec(memory_space=pl.ANY), vmem, vmem),
         scratch_shapes=[
             pltpu.SMEM((n_dest,), jnp.int32),
             pltpu.VMEM(blocks.shape, blocks.dtype),
+            pltpu.VMEM(field.shape, field.dtype),
             pltpu.VMEM((16, width), blocks.dtype),
             pltpu.SemaphoreType.DMA((n_blocks,)),
             pltpu.SemaphoreType.DMA((n_blocks,)),
             pltpu.SemaphoreType.DMA((n_dest * cap,)),
+            pltpu.SemaphoreType.DMA,
         ],
         name="pack_blocks",
-    )(target_sector, blocks)
+    )(target_sector, blocks, field)
 
 
 def block_mask():
@@ -181,41 +203,38 @@
 
 
 def tile_kernel(
-    half_ref, recv_hbm, self_ref, norm_ref, inner_ref, outer_ref, table_hbm, xt_ref,
+    half_ref, recv_ref, self_ref, norm_ref, inner_ref, outer_ref, table_hbm, xt_ref,
     state_ref, keep_ref, give_ref,
-    recv_ref, head_ref, table_ref,
+    table_ref,
     x_s, f_s, p_s, d_s, h_s, m_s, l_s, peak_s, up_s, row_s, in_s, out_s, order_s, live_v, live_s, sem,
 ):
-    n_slots, block_len, _ = recv_hbm.shape
+    n_slots, block_len, _ = recv_ref.shape
     rows = CHUNK_BLOCKS * block_len
     f32 = jnp.float32
     bf16 = jnp.bfloat16
 
-    head_copy = pltpu.make_async_copy(
-        recv_hbm.at[:, pl.ds(0, head_ref.shape[1]), pl.ds(0, head_ref.shape[2])], head_ref, sem.at[1]
-    )
-    recv_copy = pltpu.make_async_copy(recv_hbm, recv_ref, sem.at[2])
-    table_copy = pltpu.make_async_copy(table_hbm.at[pl.ds(0, TABLE_ROWS)], table_ref, sem.at[3])
-    head_copy.start()
-    recv_copy.start()
-    table_copy.start()
+    early = GROUPS * LANES
+    early_rows = pl.ds(0, early)
+    late_rows = pl.ds(early, TABLE_ROWS - early)
+    early_copy = pltpu.make_async_copy(table_hbm.at[early_rows], table_ref.at[early_rows], sem.at[1])
+    late_copy = pltpu.make_async_copy(table_hbm.at[late_rows], table_ref.at[late_rows], sem.at[2])
+    early_copy.start()
+    late_copy.start()
+    for i in range(n_slots):
+        head = recv_ref[i, 0:16, 0:128].astype(f32)
+        live_v[i : i + 1, :] = jnp.where(head[0:1, :] < MARK / 2, 1, 0)
+    flags = pltpu.make_async_copy(live_v, live_s, sem.at[0])
+    flags.start()
     l_s[...] = jnp.ones_like(l_s)
     up_s[...] = jnp.zeros_like(up_s)
     in_s[...] = jnp.zeros_like(in_s)
     out_s[...] = jnp.zeros_like(out_s)
-    head_copy.wait()
-    for i in range(n_slots):
-        head = head_ref[i].astype(f32)
-        live_v[i : i + 1, :] = jnp.where(head[0:1, :] < MARK / 2, 1, 0)
-    flags = pltpu.make_async_copy(live_v, live_s, sem.at[0])
-    flags.start()
     flags.wait()
     count = jnp.int32(0)
     for i in range(n_slots):
         order_s[count] = i
         count = count + live_s[i, 0]
-    recv_copy.wait()
-    table_copy.wait()
+    early_copy.wait()
     n_chunks = (count + CHUNK_BLOCKS - 1) // CHUNK_BLOCKS
 
     norm = norm_ref[...]
@@ -286,6 +305,7 @@
 
     lax.fori_loop(0, n_chunks, forward, 0)
 
+    late_copy.wait()
     mask = block_mask()
     inverse = 1.0 / l_s[...]
     peak = m_s[...]
@@ -357,13 +377,11 @@
             jax.ShapeDtypeStruct((obs_width // 2, hidden + width), jnp.bfloat16),
             jax.ShapeDtypeStruct((obs_width // 2, hidden + width), jnp.bfloat16),
         ),
-        in_specs=[pl.BlockSpec(memory_space=pltpu.SMEM), pl.BlockSpec(memory_space=pl.ANY)]
-        + [vmem] * 4
+        in_specs=[pl.BlockSpec(memory_space=pltpu.SMEM)]
+        + [vmem] * 5
         + [pl.BlockSpec(memory_space=pl.ANY), vmem],
         out_specs=(vmem, vmem, vmem),
         scratch_shapes=[
-            pltpu.VMEM(recv.shape, recv.dtype),
-            pltpu.VMEM((n_slots, 16, 128), recv.dtype),
             pltpu.VMEM((TABLE_ROWS, hidden), table.dtype),
             pltpu.VMEM((n_tokens, obs_width), jnp.bfloat16),
             pltpu.VMEM((n_tokens, width), jnp.bfloat16),
@@ -380,7 +398,7 @@
             pltpu.SMEM((n_slots + 1,), jnp.int32),
             pltpu.VMEM((n_slots, 128), jnp.int32),
             pltpu.SMEM((n_slots, 128), jnp.int32),
-            pltpu.SemaphoreType.DMA((4,)),
+            pltpu.SemaphoreType.DMA((3,)),
         ],
         compiler_params=pltpu.CompilerParams(vmem_limit_bytes=44 * 1024 * 1024),
         name="tile_step",
@@ -457,9 +475,11 @@
     cell_cols = hidden_member_fields.shape[2]
     n_cells = cell_rows * cell_cols
     cap_slots = max(2, 2 * block_count // lon_count)
-    send_blocks = pack_blocks(target_sector, measured_inputs, lon_count, cap_slots)
+    send_blocks, first_edge, last_edge = pack_blocks(
+        target_sector, measured_inputs, analysis_adjoint[0], lon_count, cap_slots
+    )
     obs_blocks = lax.all_to_all(send_blocks, "lon", split_axis=0, concat_axis=0, tiled=True)
-    cot_padded = extended(analysis_adjoint[0], (("lon", 1), ("lat", 0)), 1)
+    cot_padded = extended(analysis_adjoint[0], (("lon", 1), ("lat", 0)), 1, (first_edge, last_edge))
     lat_index = lax.axis_index("lat")
     row_ids = lax.broadcasted_iota(jnp.int32, (cell_rows + 2, 1, 1), 0)
     outside = ((row_ids == 0) & (lat_index == 0)) | (

time: 120 us -> 120 us (level)
    ppermute x4 -> x3, waiting for transfers between devices: 27.7 us -> 5.33 us  [extended(): lax.ppermute(lax.slice_in_dim(block, block.shape[dim] - width, None, axis...]
    ppermute x0 -> x2, waiting for transfers between devices: none -> 21.9 us  [the longest x1 21.9 us: extended(): low = lax.ppermute(edges[1], axis, forward)[:, None]]
    ppermute x0 -> x2, starting transfers between devices: none -> 4.21 us  [the longest x1 2.67 us: extended(): high = lax.ppermute(edges[0], axis, backward)[:, None]]
    ppermute x4 -> x3, starting transfers between devices: 11.9 us -> 9.46 us  [extended(): lax.ppermute(lax.slice_in_dim(block, 0, width, axis=dim), axis, backward)]
    ppermute x4 -> x3, starting transfers between devices: 5.95 us -> 4.36 us  [extended(): lax.ppermute(lax.slice_in_dim(block, block.shape[dim] - width, None, axis...]
where the time goes in v1:
time: 120 us; the launch traced here: 118 us
  blocking collectives  36.7 us (31%)
  starting transfers between devices  31.1 us (26%)
  waiting for transfers between devices  28.8 us (24%)
  Pallas kernels  17.9 us (15%)
  other arithmetic  1.37 us (1%)
    all_to_all x1, blocking collectives, reduce_everywhere(): lax.all_to_all(pair.reshape(lon_count, n_rows // lon_count, n_cols), 'lon...  22 us
    ppermute x1, waiting for transfers between devices, extended(): low = lax.ppermute(edges[1], axis, forward)[:, None]  21.9 us
    all_to_all x1, blocking collectives, reduce_everywhere(): lax.all_to_all(jnp.broadcast_to(part[None], (lat_count,) + part.shape), '...  14.7 us
    pallas_call x1, Pallas kernels, tile_step(): pl.pallas_call(tile_kernel, out_shape=(jax.ShapeDtypeStruct((n_cells, wid...  11.1 us
    ppermute x3, starting transfers between devices, extended(): lax.ppermute(lax.slice_in_dim(block, 0, width, axis=dim), axis, backward)  9.46 us
    all_to_all x1, starting transfers between devices, per_device(): lax.all_to_all(send_blocks, 'lon', split_axis=0, concat_axis=0, tiled=True)  7.62 us
    all_to_all x1, starting transfers between devices, reduce_everywhere(): lax.all_to_all(jnp.broadcast_to(total[None], (lon_count,) + total.shape),...  5.35 us
    ppermute x3, waiting for transfers between devices, extended(): lax.ppermute(lax.slice_in_dim(block, block.shape[dim] - width, None, axis...  5.33 us
  transfers between devices with their start and end apart: 12, of which 5 were waited for; matrix products, arithmetic and copies ran while one was open for 1% of the time, Pallas kernels for 2%

profile of v1, /device:TPU:2, one launch (start us, length us, event | category | flops | bytes accessed | tf_op | source)
XLA Modules:
  0.0 117.8 jit_solution(14824872519445841709)
XLA Ops:
  0.6 3.8 %pack_blocks.1 = (bf16[16,2,128,256]{3,2,1,0:T(8,128)(2,1)}, bf16[8,768]{1,0:T(8,128)(2,1)}, bf16[8,768]{1,0:T(8,128)(2,1)}) custom-call(s32[16]{0:T(128)} %target_ref.1, bf16[16,128,256]{2,1,0:T(8,128)(2,1)} %blocks_ref.1, bf16[8,8,768]{2,1,0:T(8,128)(2,1)} %bitcast.21), custom_call_target="tpu_custom_call" | custom-call | tf_op jit(solution)/shard_map/pack_blocks/pallas_call | solution.py:114
  4.5 7.6 %all-to-all-start = ((bf16[16,2,128,256]{3,2,1,0:T(8,128)(2,1)}), bf16[16,2,128,256]{3,2,1,0:T(8,128)(2,1)S(1)}, u32[]{:S(2)}, u32[]{:S(2)}) async-start(bf16[16,2,128,256]{3,2,1,0:T(8,128)(2,1)} %get-tuple-element.14), calls=%async_computation | async-start | bytes 4194304 | tf_op jit(solution)/shard_map/all_to_all | solution.py:481
  12.2 1.5 %collective-permute-start = (bf16[8,768]{1,0:T(8,128)(2,1)S(1)}, bf16[8,768]{1,0:T(8,128)(2,1)S(1)}, u32[]{:S(2)}, u32[]{:S(2)}) collective-permute-start(bf16[8,768]{1,0:T(8,128)(2,1)S(1)} %copy-done.7), channel_id=1, source_target_pairs={{0,2},{2,4},{4,6},{6,8},{8,10},{10,12},{12,14},{14,16},{16,18},{18... | collective-permute-start | bytes 36872 | tf_op jit(solution)/shard_map/ppermute | solution.py:31
  13.7 2.7 %collective-permute-start.1 = (bf16[8,768]{1,0:T(8,128)(2,1)S(1)}, bf16[8,768]{1,0:T(8,128)(2,1)S(1)}, u32[]{:S(2)}, u32[]{:S(2)}) collective-permute-start(bf16[8,768]{1,0:T(8,128)(2,1)S(1)} %copy-done.6), channel_id=1, source_target_pairs={{2,0},{4,2},{6,4},{8,6},{10,8},{12,10},{14,12},{16,14},{18,16},{20... | collective-permute-start | bytes 36872 | tf_op jit(solution)/shard_map/ppermute | solution.py:32
  16.5 21.9 %collective-permute-done = bf16[8,768]{1,0:T(8,128)(2,1)S(1)} collective-permute-done((bf16[8,768]{1,0:T(8,128)(2,1)S(1)}, bf16[8,768]{1,0:T(8,128)(2,1)S(1)}, u32[]{:S(2)}, u32[]{:S(2)}) %collective-permute-start) | collective-permute-done | bytes 12320 | tf_op jit(solution)/shard_map/ppermute | solution.py:31
  38.5 2.0 %collective-permute-start.2 = (bf16[1,10,768]{2,1,0:T(8,128)(2,1)S(1)}, bf16[1,10,768]{2,1,0:T(8,128)(2,1)S(1)}, u32[]{:S(2)}, u32[]{:S(2)}) collective-permute-start(bf16[1,10,768]{2,1,0:T(8,128)(2,1)S(1)} %get-tuple-element.35), channel_id=1, source_target_pairs={{0,32},{32,64},{64,96},{96,128},{128,160},{160,192},{192,224},{224... | collective-permute-start | bytes 46088 | tf_op jit(solution)/shard_map/ppermute | solution.py:35
  40.5 4.1 %collective-permute-start.3 = (bf16[1,10,768]{2,1,0:T(8,128)(2,1)S(1)}, bf16[1,10,768]{2,1,0:T(8,128)(2,1)S(1)}, u32[]{:S(2)}, u32[]{:S(2)}) collective-permute-start(bf16[1,10,768]{2,1,0:T(8,128)(2,1)S(1)} %get-tuple-element.36), channel_id=1, source_target_pairs={{32,0},{64,32},{96,64},{128,96},{160,128},{192,160},{224,192},{0,2... | collective-permute-start | bytes 46088 | tf_op jit(solution)/shard_map/ppermute | solution.py:38
  44.8 1.6 %collective-permute-done.2 = bf16[1,10,768]{2,1,0:T(8,128)(2,1)S(1)} collective-permute-done((bf16[1,10,768]{2,1,0:T(8,128)(2,1)S(1)}, bf16[1,10,768]{2,1,0:T(8,128)(2,1)S(1)}, u32[]{:S(2)}, u32[]{:S(2)}) %collective-permute-start.2) | collective-permute-done | bytes 15392 | tf_op jit(solution)/shard_map/ppermute | solution.py:35
  46.4 0.2 fusion.19.grad_ref
  46.6 2.0 %prepare_cells.1 = (bf16[153600,256]{1,0:T(8,128)(2,1)}, f32[3,256,256]{2,1,0:T(8,128)S(1)}, f32[2,768]{1,0:T(2,128)S(1)}) custom-call(bf16[64,768]{1,0:T(8,128)(2,1)S(1)} %bitcast.20, bf16[64,768]{1,0:T(8,128)(2,1)S(1)} %fusion.19.grad_ref, bf16[768,768]{1,0:T(8,128)(2,1)S(1)} %copy-done.1, bf16[256,768]{1,0:T(8,128)(2,1)S(1)} %copy-done), custom_call_target="tpu_custom_call" | custom-call | tf_op jit(solution)/shard_map/prepare_cells/pallas_call | solution.py:187
  48.7 11.1 %tile_step.1 = (bf16[64,768]{1,0:T(8,128)(2,1)S(1)}, bf16[128,1024]{1,0:T(8,128)(2,1)S(1)}, bf16[128,1024]{1,0:T(8,128)(2,1)S(1)}) custom-call(s32[1]{0:T(128)} %bitcast.half_ref, bf16[32,128,256]{2,1,0:T(8,128)(2,1)S(1)} %bitcast.14, f32[2,768]{1,0:T(2,128)S(1)} %get-tuple-element.17.self_ref, f32[1,768]{1,0:T(1,128)S(1)} %broadcast_in_dim_reshape.3.norm_ref, ...), custom_call_target="tpu_custom_call" | custom-call | tf_op jit(solution)/shard_map/tile_step/pallas_call | solution.py:373
  59.8 1.5 %collective-permute-done.8 = bf16[128,1024]{1,0:T(8,128)(2,1)S(1)} collective-permute-done((bf16[128,1024]{1,0:T(8,128)(2,1)S(1)}, bf16[128,1024]{1,0:T(8,128)(2,1)S(1)}, u32[]{:S(2)}, u32[]{:S(2)}) %collective-permute-start.8) | collective-permute-done | bytes 262176 | tf_op jit(solution)/shard_map/ppermute | solution.py:441
  61.4 22.0 %all_to_all.20 = bf16[16,8,1024]{2,1,0:T(8,128)(2,1)S(1)} all-to-all(bf16[16,8,1024]{2,1,0:T(8,128)(2,1)S(1)} %fusion), channel_id=1, replica_groups=mesh['lat'=8,'lon'=16,'mem'=2] {'lon'}, dimensions={0} | all-to-all | bytes 524288 | tf_op jit(solution)/shard_map/all_to_all | solution.py:443
  83.5 14.7 %all_to_all.21 = bf16[8,8,1024]{2,1,0:T(8,128)(2,1)S(1)} all-to-all(bf16[8,8,1024]{2,1,0:T(8,128)(2,1)S(1)} %broadcast_in_dim.34), channel_id=1, replica_groups=mesh['lat'=8,'lon'=16,'mem'=2] {'lat'}, dimensions={0} | all-to-all | bytes 262144 | tf_op jit(solution)/shard_map/all_to_all | solution.py:447
  98.2 0.7 broadcast_in_dim.35
  99.0 5.3 %all-to-all-start.3 = ((bf16[16,8,1024]{2,1,0:T(8,128)(2,1)}), bf16[16,8,1024]{2,1,0:T(8,128)(2,1)S(1)}, u32[]{:S(2)}, u32[]{:S(2)}) async-start(bf16[16,8,1024]{2,1,0:T(8,128)(2,1)} %broadcast_in_dim.35), calls=%async_computation.3 | async-start | bytes 524288 | tf_op jit(solution)/shard_map/all_to_all | solution.py:451
  104.3 1.7 %collective-permute-start.4 = (bf16[8,1,768]{2,1,0:T(2,128)(2,1)S(1)}, bf16[8,1,768]{2,1,0:T(2,128)(2,1)S(1)}, u32[]{:S(2)}, u32[]{:S(2)}) collective-permute-start(bf16[8,1,768]{2,1,0:T(2,128)(2,1)S(1)} %get-tuple-element.37), channel_id=1, source_target_pairs={{0,2},{2,4},{4,6},{6,8},{8,10},{10,12},{12,14},{14,16},{16,18},{18... | collective-permute-start | bytes 36872 | tf_op jit(solution)/shard_map/ppermute | solution.py:35
  106.1 2.7 %collective-permute-start.5 = (bf16[8,1,768]{2,1,0:T(2,128)(2,1)S(1)}, bf16[8,1,768]{2,1,0:T(2,128)(2,1)S(1)}, u32[]{:S(2)}, u32[]{:S(2)}) collective-permute-start(bf16[8,1,768]{2,1,0:T(2,128)(2,1)S(1)} %get-tuple-element.38), channel_id=1, source_target_pairs={{2,0},{4,2},{6,4},{8,6},{10,8},{12,10},{14,12},{16,14},{18,16},{20... | collective-permute-start | bytes 36872 | tf_op jit(solution)/shard_map/ppermute | solution.py:38
  108.7 2.0 %collective-permute-done.4 = bf16[8,1,768]{2,1,0:T(2,128)(2,1)S(1)} collective-permute-done((bf16[8,1,768]{2,1,0:T(2,128)(2,1)S(1)}, bf16[8,1,768]{2,1,0:T(2,128)(2,1)S(1)}, u32[]{:S(2)}, u32[]{:S(2)}) %collective-permute-start.4) | collective-permute-done | bytes 12320 | tf_op jit(solution)/shard_map/ppermute | solution.py:35
  110.8 0.6 collective-permute-start.6
  111.4 2.7 %collective-permute-start.7 = (bf16[1,10,768]{2,1,0:T(8,128)(2,1)S(1)}, bf16[1,10,768]{2,1,0:T(8,128)(2,1)S(1)}, u32[]{:S(2)}, u32[]{:S(2)}) collective-permute-start(bf16[1,10,768]{2,1,0:T(8,128)(2,1)S(1)} %get-tuple-element.34), channel_id=1, source_target_pairs={{32,0},{64,32},{96,64},{128,96},{160,128},{192,160},{224,192},{0,2... | collective-permute-start | bytes 46088 | tf_op jit(solution)/shard_map/ppermute | solution.py:38
  114.1 1.8 %collective-permute-done.6 = bf16[1,10,768]{2,1,0:T(8,128)(2,1)S(1)} collective-permute-done((bf16[1,10,768]{2,1,0:T(8,128)(2,1)S(1)}, bf16[1,10,768]{2,1,0:T(8,128)(2,1)S(1)}, u32[]{:S(2)}, u32[]{:S(2)}) %collective-permute-start.6) | collective-permute-done | bytes 15392 | tf_op jit(solution)/shard_map/ppermute | solution.py:35
  116.0 0.8 fusion.20
  116.8 1.0 unfold.1
  (43 shorter events, 0.9 us)
Async XLA Ops:
  4.5 7.7 %copy-start.7 = (bf16[8,768]{1,0:T(8,128)(2,1)S(1)}, bf16[8,768]{1,0:T(8,128)(2,1)}, u32[]{:S(2)}) copy-start(bf16[8,768]{1,0:T(8,128)(2,1)} %get-tuple-element.15) | copy-start | bytes 36868
  4.5 9.2 %copy-start.6 = (bf16[8,768]{1,0:T(8,128)(2,1)S(1)}, bf16[8,768]{1,0:T(8,128)(2,1)}, u32[]{:S(2)}) copy-start(bf16[8,768]{1,0:T(8,128)(2,1)} %get-tuple-element.16) | copy-start | bytes 36868
  4.5 11.9 %copy-start.8 = (f32[12]{0:T(128)S(1)}, f32[12]{0:T(128)}, u32[]{:S(2)}) copy-start(f32[12]{0:T(128)} %param.16) | copy-start | bytes 148
  4.5 11.9 %copy-start.5 = (f32[8,768]{1,0:T(8,128)S(1)}, f32[8,768]{1,0:T(8,128)}, u32[]{:S(2)}) copy-start(f32[8,768]{1,0:T(8,128)} %param.17) | copy-start | bytes 73732
  4.5 33.9 %copy-start.4 = (bf16[1,8,8,768]{3,2,1,0:T(8,128)(2,1)S(1)}, bf16[1,8,8,768]{3,2,1,0:T(8,128)(2,1)}, u32[]{:S(2)}) copy-start(bf16[1,8,8,768]{3,2,1,0:T(8,128)(2,1)} %param.12) | copy-start | bytes 294916
  4.5 44.1 %all-to-all-start = ((bf16[16,2,128,256]{3,2,1,0:T(8,128)(2,1)}), bf16[16,2,128,256]{3,2,1,0:T(8,128)(2,1)S(1)}, u32[]{:S(2)}, u32[]{:S(2)}) async-start(bf16[16,2,128,256]{3,2,1,0:T(8,128)(2,1)} %get-tuple-element.14), calls=%async_computation | async-start | bytes 4194304 | tf_op jit(solution)/shard_map/all_to_all | solution.py:481
  12.1 34.5 %copy-start = (bf16[256,768]{1,0:T(8,128)(2,1)S(1)}, bf16[256,768]{1,0:T(8,128)(2,1)}, u32[]{:S(2)}) copy-start(bf16[256,768]{1,0:T(8,128)(2,1)} %outer_ref.3) | copy-start | bytes 1179652
  12.1 34.5 %copy-start.3 = (bf16[1,8,8,768]{3,2,1,0:T(8,128)(2,1)S(1)}, bf16[1,8,8,768]{3,2,1,0:T(8,128)(2,1)}, u32[]{:S(2)}) copy-start(bf16[1,8,8,768]{3,2,1,0:T(8,128)(2,1)} %param.11) | copy-start | bytes 294916
  12.2 26.2 %collective-permute-start = (bf16[8,768]{1,0:T(8,128)(2,1)S(1)}, bf16[8,768]{1,0:T(8,128)(2,1)S(1)}, u32[]{:S(2)}, u32[]{:S(2)}) collective-permute-start(bf16[8,768]{1,0:T(8,128)(2,1)S(1)} %copy-done.7), channel_id=1, source_target_pairs={{0,2},{2,4},{4,6},{6,8},{8,10},{10,12},{12,14},{14,16},{16,18},{18... | collective-permute-start | bytes 36872 | tf_op jit(solution)/shard_map/ppermute | solution.py:31
  13.7 24.7 %collective-permute-start.1 = (bf16[8,768]{1,0:T(8,128)(2,1)S(1)}, bf16[8,768]{1,0:T(8,128)(2,1)S(1)}, u32[]{:S(2)}, u32[]{:S(2)}) collective-permute-start(bf16[8,768]{1,0:T(8,128)(2,1)S(1)} %copy-done.6), channel_id=1, source_target_pairs={{2,0},{4,2},{6,4},{8,6},{10,8},{12,10},{14,12},{16,14},{18,16},{20... | collective-permute-start | bytes 36872 | tf_op jit(solution)/shard_map/ppermute | solution.py:32
  38.5 7.8 %collective-permute-start.2 = (bf16[1,10,768]{2,1,0:T(8,128)(2,1)S(1)}, bf16[1,10,768]{2,1,0:T(8,128)(2,1)S(1)}, u32[]{:S(2)}, u32[]{:S(2)}) collective-permute-start(bf16[1,10,768]{2,1,0:T(8,128)(2,1)S(1)} %get-tuple-element.35), channel_id=1, source_target_pairs={{0,32},{32,64},{64,96},{96,128},{128,160},{160,192},{192,224},{224... | collective-permute-start | bytes 46088 | tf_op jit(solution)/shard_map/ppermute | solution.py:35
  40.5 5.8 %collective-permute-start.3 = (bf16[1,10,768]{2,1,0:T(8,128)(2,1)S(1)}, bf16[1,10,768]{2,1,0:T(8,128)(2,1)S(1)}, u32[]{:S(2)}, u32[]{:S(2)}) collective-permute-start(bf16[1,10,768]{2,1,0:T(8,128)(2,1)S(1)} %get-tuple-element.36), channel_id=1, source_target_pairs={{32,0},{64,32},{96,64},{128,96},{160,128},{192,160},{224,192},{0,2... | collective-permute-start | bytes 46088 | tf_op jit(solution)/shard_map/ppermute | solution.py:38
  44.8 1.9 %copy-start.1 = (bf16[768,768]{1,0:T(8,128)(2,1)S(1)}, bf16[768,768]{1,0:T(8,128)(2,1)}, u32[]{:S(2)}) copy-start(bf16[768,768]{1,0:T(8,128)(2,1)} %probe_ref.1) | copy-start | bytes 3538948
  44.8 3.9 %copy-start.2 = (bf16[256,256]{1,0:T(8,128)(2,1)S(1)}, bf16[256,256]{1,0:T(8,128)(2,1)}, u32[]{:S(2)}) copy-start(bf16[256,256]{1,0:T(8,128)(2,1)} %inner_ref.1) | copy-start | bytes 393220
  59.7 1.6 %collective-permute-start.8 = (bf16[128,1024]{1,0:T(8,128)(2,1)S(1)}, bf16[128,1024]{1,0:T(8,128)(2,1)S(1)}, u32[]{:S(2)}, u32[]{:S(2)}) collective-permute-start(bf16[128,1024]{1,0:T(8,128)(2,1)S(1)} %get-tuple-element.22), channel_id=1, source_target_pairs={{0,1},{1,0},{2,3},{3,2},{4,5},{5,4},{6,7},{7,6},{8,9},{9,8},{10,11... | collective-permute-start | bytes 786440 | tf_op jit(solution)/shard_map/ppermute | solution.py:441
  99.0 15.1 %all-to-all-start.3 = ((bf16[16,8,1024]{2,1,0:T(8,128)(2,1)}), bf16[16,8,1024]{2,1,0:T(8,128)(2,1)S(1)}, u32[]{:S(2)}, u32[]{:S(2)}) async-start(bf16[16,8,1024]{2,1,0:T(8,128)(2,1)} %broadcast_in_dim.35), calls=%async_computation.3 | async-start | bytes 524288 | tf_op jit(solution)/shard_map/all_to_all | solution.py:451
  104.3 6.4 %collective-permute-start.4 = (bf16[8,1,768]{2,1,0:T(2,128)(2,1)S(1)}, bf16[8,1,768]{2,1,0:T(2,128)(2,1)S(1)}, u32[]{:S(2)}, u32[]{:S(2)}) collective-permute-start(bf16[8,1,768]{2,1,0:T(2,128)(2,1)S(1)} %get-tuple-element.37), channel_id=1, source_target_pairs={{0,2},{2,4},{4,6},{6,8},{8,10},{10,12},{12,14},{14,16},{16,18},{18... | collective-permute-start | bytes 36872 | tf_op jit(solution)/shard_map/ppermute | solution.py:35
  106.1 4.7 %collective-permute-start.5 = (bf16[8,1,768]{2,1,0:T(2,128)(2,1)S(1)}, bf16[8,1,768]{2,1,0:T(2,128)(2,1)S(1)}, u32[]{:S(2)}, u32[]{:S(2)}) collective-permute-start(bf16[8,1,768]{2,1,0:T(2,128)(2,1)S(1)} %get-tuple-element.38), channel_id=1, source_target_pairs={{2,0},{4,2},{6,4},{8,6},{10,8},{12,10},{14,12},{16,14},{18,16},{20... | collective-permute-start | bytes 36872 | tf_op jit(solution)/shard_map/ppermute | solution.py:38
  110.8 5.1 %collective-permute-start.6 = (bf16[1,10,768]{2,1,0:T(8,128)(2,1)S(1)}, bf16[1,10,768]{2,1,0:T(8,128)(2,1)S(1)}, u32[]{:S(2)}, u32[]{:S(2)}) collective-permute-start(bf16[1,10,768]{2,1,0:T(8,128)(2,1)S(1)} %get-tuple-element.33), channel_id=1, source_target_pairs={{0,32},{32,64},{64,96},{96,128},{128,160},{160,192},{192,224},{224... | collective-permute-start | bytes 46088 | tf_op jit(solution)/shard_map/ppermute | solution.py:35
  111.4 4.5 %collective-permute-start.7 = (bf16[1,10,768]{2,1,0:T(8,128)(2,1)S(1)}, bf16[1,10,768]{2,1,0:T(8,128)(2,1)S(1)}, u32[]{:S(2)}, u32[]{:S(2)}) collective-permute-start(bf16[1,10,768]{2,1,0:T(8,128)(2,1)S(1)} %get-tuple-element.34), channel_id=1, source_target_pairs={{32,0},{64,32},{96,64},{128,96},{160,128},{192,160},{224,192},{0,2... | collective-permute-start | bytes 46088 | tf_op jit(solution)/shard_map/ppermute | solution.py:38
  114.1 2.7 %collective-permute-start.9 = (bf16[128,1024]{1,0:T(8,128)(2,1)S(1)}, bf16[128,1024]{1,0:T(8,128)(2,1)S(1)}, u32[]{:S(2)}, u32[]{:S(2)}) collective-permute-start(bf16[128,1024]{1,0:T(8,128)(2,1)S(1)} %bitcast.15), channel_id=1, source_target_pairs={{0,1},{1,0},{2,3},{3,2},{4,5},{5,4},{6,7},{7,6},{8,9},{9,8},{10,11... | collective-permute-start | bytes 786440 | tf_op jit(solution)/shard_map/ppermute | solution.py:454

commit v2 on v1

--- a/solution.py
+++ b/solution.py
@@ -11,7 +11,7 @@
 CHANNELS_PER_ATT = 64
 GROUPS = 3
 LANES = 256
-CHUNK_BLOCKS = 8
+CHUNK_BLOCKS = 16
 PIECE_BLOCKS = 8
 MARK = 512.0
 TABLE_ROWS = 5 * GROUPS * LANES
@@ -75,12 +75,12 @@
     def copy_of(b, dest, slot):
         return pltpu.make_async_copy(stage_ref.at[b], send_ref.at[dest, slot], out_sem.at[b])
 
+    places = []
     for b in range(n_blocks):
         dest = target_ref[b]
         slot = count_ref[dest]
         count_ref[dest] = slot + 1
-        loads[b].wait()
-        copy_of(b, dest, slot).start()
+        places.append((dest, slot))
 
     def mark_of(d, slot):
         return pltpu.make_async_copy(
@@ -94,6 +94,9 @@
             def _():
                 mark_of(d, slot).start()
 
+    for b, (dest, slot) in enumerate(places):
+        loads[b].wait()
+        copy_of(b, dest, slot).start()
     cells.wait()
     grid = [cells_ref[row].astype(jnp.float32) for row in range(cells_ref.shape[0])]
     first_ref[...] = jnp.concatenate([row[0:1] for row in grid], axis=0).astype(first_ref.dtype)

time: 120 us -> 121 us (level)
  blocking collectives: 36.7 us -> 38.4 us
    all_to_all x1, blocking collectives: 14.7 us -> 16.8 us  [reduce_everywhere(): lax.all_to_all(jnp.broadcast_to(part[None], (lat_count,) + part.shape), '...]
where the time goes in v2:
time: 121 us; the launch traced here: 119 us
  blocking collectives  38.4 us (32%)
  starting transfers between devices  30.8 us (25%)
  waiting for transfers between devices  29 us (24%)
  Pallas kernels  17.8 us (15%)
  other arithmetic  1.37 us (1%)
    ppermute x1, waiting for transfers between devices, extended(): low = lax.ppermute(edges[1], axis, forward)[:, None]  22 us
    all_to_all x1, blocking collectives, reduce_everywhere(): lax.all_to_all(pair.reshape(lon_count, n_rows // lon_count, n_cols), 'lon...  21.6 us
    all_to_all x1, blocking collectives, reduce_everywhere(): lax.all_to_all(jnp.broadcast_to(part[None], (lat_count,) + part.shape), '...  16.8 us
    pallas_call x1, Pallas kernels, tile_step(): pl.pallas_call(tile_kernel, out_shape=(jax.ShapeDtypeStruct((n_cells, wid...  10.9 us
    ppermute x3, starting transfers between devices, extended(): lax.ppermute(lax.slice_in_dim(block, 0, width, axis=dim), axis, backward)  9.46 us
    all_to_all x1, starting transfers between devices, per_device(): lax.all_to_all(send_blocks, 'lon', split_axis=0, concat_axis=0, tiled=True)  7.58 us
    ppermute x3, waiting for transfers between devices, extended(): lax.ppermute(lax.slice_in_dim(block, block.shape[dim] - width, None, axis...  5.41 us
    all_to_all x1, starting transfers between devices, reduce_everywhere(): lax.all_to_all(jnp.broadcast_to(total[None], (lon_count,) + total.shape),...  5.34 us
  transfers between devices with their start and end apart: 12, of which 5 were waited for; matrix products, arithmetic and copies ran while one was open for 1% of the time, Pallas kernels for 2%

profile of v2, /device:TPU:2, one launch (start us, length us, event | category | flops | bytes accessed | tf_op | source)
XLA Modules:
  0.0 119.2 jit_solution(16974751175809912239)
XLA Ops:
  0.6 3.9 %pack_blocks.1 = (bf16[16,2,128,256]{3,2,1,0:T(8,128)(2,1)}, bf16[8,768]{1,0:T(8,128)(2,1)}, bf16[8,768]{1,0:T(8,128)(2,1)}) custom-call(s32[16]{0:T(128)} %target_ref.1, bf16[16,128,256]{2,1,0:T(8,128)(2,1)} %blocks_ref.1, bf16[8,8,768]{2,1,0:T(8,128)(2,1)} %bitcast.21), custom_call_target="tpu_custom_call" | custom-call | tf_op jit(solution)/shard_map/pack_blocks/pallas_call | solution.py:117
  4.6 7.6 %all-to-all-start = ((bf16[16,2,128,256]{3,2,1,0:T(8,128)(2,1)}), bf16[16,2,128,256]{3,2,1,0:T(8,128)(2,1)S(1)}, u32[]{:S(2)}, u32[]{:S(2)}) async-start(bf16[16,2,128,256]{3,2,1,0:T(8,128)(2,1)} %get-tuple-element.14), calls=%async_computation | async-start | bytes 4194304 | tf_op jit(solution)/shard_map/all_to_all | solution.py:484
  12.2 1.5 %collective-permute-start = (bf16[8,768]{1,0:T(8,128)(2,1)S(1)}, bf16[8,768]{1,0:T(8,128)(2,1)S(1)}, u32[]{:S(2)}, u32[]{:S(2)}) collective-permute-start(bf16[8,768]{1,0:T(8,128)(2,1)S(1)} %copy-done.7), channel_id=1, source_target_pairs={{0,2},{2,4},{4,6},{6,8},{8,10},{10,12},{12,14},{14,16},{16,18},{18... | collective-permute-start | bytes 36872 | tf_op jit(solution)/shard_map/ppermute | solution.py:31
  13.7 2.7 %collective-permute-start.1 = (bf16[8,768]{1,0:T(8,128)(2,1)S(1)}, bf16[8,768]{1,0:T(8,128)(2,1)S(1)}, u32[]{:S(2)}, u32[]{:S(2)}) collective-permute-start(bf16[8,768]{1,0:T(8,128)(2,1)S(1)} %copy-done.6), channel_id=1, source_target_pairs={{2,0},{4,2},{6,4},{8,6},{10,8},{12,10},{14,12},{16,14},{18,16},{20... | collective-permute-start | bytes 36872 | tf_op jit(solution)/shard_map/ppermute | solution.py:32
  16.5 22.0 %collective-permute-done = bf16[8,768]{1,0:T(8,128)(2,1)S(1)} collective-permute-done((bf16[8,768]{1,0:T(8,128)(2,1)S(1)}, bf16[8,768]{1,0:T(8,128)(2,1)S(1)}, u32[]{:S(2)}, u32[]{:S(2)}) %collective-permute-start) | collective-permute-done | bytes 12320 | tf_op jit(solution)/shard_map/ppermute | solution.py:31
  38.6 1.9 %collective-permute-start.2 = (bf16[1,10,768]{2,1,0:T(8,128)(2,1)S(1)}, bf16[1,10,768]{2,1,0:T(8,128)(2,1)S(1)}, u32[]{:S(2)}, u32[]{:S(2)}) collective-permute-start(bf16[1,10,768]{2,1,0:T(8,128)(2,1)S(1)} %get-tuple-element.35), channel_id=1, source_target_pairs={{0,32},{32,64},{64,96},{96,128},{128,160},{160,192},{192,224},{224... | collective-permute-start | bytes 46088 | tf_op jit(solution)/shard_map/ppermute | solution.py:35
  40.6 4.1 %collective-permute-start.3 = (bf16[1,10,768]{2,1,0:T(8,128)(2,1)S(1)}, bf16[1,10,768]{2,1,0:T(8,128)(2,1)S(1)}, u32[]{:S(2)}, u32[]{:S(2)}) collective-permute-start(bf16[1,10,768]{2,1,0:T(8,128)(2,1)S(1)} %get-tuple-element.36), channel_id=1, source_target_pairs={{32,0},{64,32},{96,64},{128,96},{160,128},{192,160},{224,192},{0,2... | collective-permute-start | bytes 46088 | tf_op jit(solution)/shard_map/ppermute | solution.py:38
  44.8 1.6 %collective-permute-done.2 = bf16[1,10,768]{2,1,0:T(8,128)(2,1)S(1)} collective-permute-done((bf16[1,10,768]{2,1,0:T(8,128)(2,1)S(1)}, bf16[1,10,768]{2,1,0:T(8,128)(2,1)S(1)}, u32[]{:S(2)}, u32[]{:S(2)}) %collective-permute-start.2) | collective-permute-done | bytes 15392 | tf_op jit(solution)/shard_map/ppermute | solution.py:35
  46.5 0.2 fusion.19.grad_ref
  46.7 2.0 %prepare_cells.1 = (bf16[153600,256]{1,0:T(8,128)(2,1)}, f32[3,256,256]{2,1,0:T(8,128)S(1)}, f32[2,768]{1,0:T(2,128)S(1)}) custom-call(bf16[64,768]{1,0:T(8,128)(2,1)S(1)} %bitcast.20, bf16[64,768]{1,0:T(8,128)(2,1)S(1)} %fusion.19.grad_ref, bf16[768,768]{1,0:T(8,128)(2,1)S(1)} %copy-done.1, bf16[256,768]{1,0:T(8,128)(2,1)S(1)} %copy-done), custom_call_target="tpu_custom_call" | custom-call | tf_op jit(solution)/shard_map/prepare_cells/pallas_call | solution.py:190
  48.7 10.9 %tile_step.1 = (bf16[64,768]{1,0:T(8,128)(2,1)S(1)}, bf16[128,1024]{1,0:T(8,128)(2,1)S(1)}, bf16[128,1024]{1,0:T(8,128)(2,1)S(1)}) custom-call(s32[1]{0:T(128)} %bitcast.half_ref, bf16[32,128,256]{2,1,0:T(8,128)(2,1)S(1)} %bitcast.14, f32[2,768]{1,0:T(2,128)S(1)} %get-tuple-element.17.self_ref, f32[1,768]{1,0:T(1,128)S(1)} %broadcast_in_dim_reshape.3.norm_ref, ...), custom_call_target="tpu_custom_call" | custom-call | tf_op jit(solution)/shard_map/tile_step/pallas_call | solution.py:376
  59.7 1.5 %collective-permute-done.8 = bf16[128,1024]{1,0:T(8,128)(2,1)S(1)} collective-permute-done((bf16[128,1024]{1,0:T(8,128)(2,1)S(1)}, bf16[128,1024]{1,0:T(8,128)(2,1)S(1)}, u32[]{:S(2)}, u32[]{:S(2)}) %collective-permute-start.8) | collective-permute-done | bytes 262176 | tf_op jit(solution)/shard_map/ppermute | solution.py:444
  61.3 21.6 %all_to_all.20 = bf16[16,8,1024]{2,1,0:T(8,128)(2,1)S(1)} all-to-all(bf16[16,8,1024]{2,1,0:T(8,128)(2,1)S(1)} %fusion), channel_id=1, replica_groups=mesh['lat'=8,'lon'=16,'mem'=2] {'lon'}, dimensions={0} | all-to-all | bytes 524288 | tf_op jit(solution)/shard_map/all_to_all | solution.py:446
  83.0 16.8 %all_to_all.21 = bf16[8,8,1024]{2,1,0:T(8,128)(2,1)S(1)} all-to-all(bf16[8,8,1024]{2,1,0:T(8,128)(2,1)S(1)} %broadcast_in_dim.34), channel_id=1, replica_groups=mesh['lat'=8,'lon'=16,'mem'=2] {'lat'}, dimensions={0} | all-to-all | bytes 262144 | tf_op jit(solution)/shard_map/all_to_all | solution.py:450
  99.8 0.7 broadcast_in_dim.35
  100.5 5.3 %all-to-all-start.3 = ((bf16[16,8,1024]{2,1,0:T(8,128)(2,1)}), bf16[16,8,1024]{2,1,0:T(8,128)(2,1)S(1)}, u32[]{:S(2)}, u32[]{:S(2)}) async-start(bf16[16,8,1024]{2,1,0:T(8,128)(2,1)} %broadcast_in_dim.35), calls=%async_computation.3 | async-start | bytes 524288 | tf_op jit(solution)/shard_map/all_to_all | solution.py:454
  105.9 1.5 %collective-permute-start.4 = (bf16[8,1,768]{2,1,0:T(2,128)(2,1)S(1)}, bf16[8,1,768]{2,1,0:T(2,128)(2,1)S(1)}, u32[]{:S(2)}, u32[]{:S(2)}) collective-permute-start(bf16[8,1,768]{2,1,0:T(2,128)(2,1)S(1)} %get-tuple-element.37), channel_id=1, source_target_pairs={{0,2},{2,4},{4,6},{6,8},{8,10},{10,12},{12,14},{14,16},{16,18},{18... | collective-permute-start | bytes 36872 | tf_op jit(solution)/shard_map/ppermute | solution.py:35
  107.4 2.7 %collective-permute-start.5 = (bf16[8,1,768]{2,1,0:T(2,128)(2,1)S(1)}, bf16[8,1,768]{2,1,0:T(2,128)(2,1)S(1)}, u32[]{:S(2)}, u32[]{:S(2)}) collective-permute-start(bf16[8,1,768]{2,1,0:T(2,128)(2,1)S(1)} %get-tuple-element.38), channel_id=1, source_target_pairs={{2,0},{4,2},{6,4},{8,6},{10,8},{12,10},{14,12},{16,14},{18,16},{20... | collective-permute-start | bytes 36872 | tf_op jit(solution)/shard_map/ppermute | solution.py:38
  110.1 2.1 %collective-permute-done.4 = bf16[8,1,768]{2,1,0:T(2,128)(2,1)S(1)} collective-permute-done((bf16[8,1,768]{2,1,0:T(2,128)(2,1)S(1)}, bf16[8,1,768]{2,1,0:T(2,128)(2,1)S(1)}, u32[]{:S(2)}, u32[]{:S(2)}) %collective-permute-start.4) | collective-permute-done | bytes 12320 | tf_op jit(solution)/shard_map/ppermute | solution.py:35
  112.2 0.6 collective-permute-start.6
  112.8 2.7 %collective-permute-start.7 = (bf16[1,10,768]{2,1,0:T(8,128)(2,1)S(1)}, bf16[1,10,768]{2,1,0:T(8,128)(2,1)S(1)}, u32[]{:S(2)}, u32[]{:S(2)}) collective-permute-start(bf16[1,10,768]{2,1,0:T(8,128)(2,1)S(1)} %get-tuple-element.34), channel_id=1, source_target_pairs={{32,0},{64,32},{96,64},{128,96},{160,128},{192,160},{224,192},{0,2... | collective-permute-start | bytes 46088 | tf_op jit(solution)/shard_map/ppermute | solution.py:38
  115.5 1.8 %collective-permute-done.6 = bf16[1,10,768]{2,1,0:T(8,128)(2,1)S(1)} collective-permute-done((bf16[1,10,768]{2,1,0:T(8,128)(2,1)S(1)}, bf16[1,10,768]{2,1,0:T(8,128)(2,1)S(1)}, u32[]{:S(2)}, u32[]{:S(2)}) %collective-permute-start.6) | collective-permute-done | bytes 15392 | tf_op jit(solution)/shard_map/ppermute | solution.py:35
  117.4 0.8 fusion.20
  118.2 1.0 unfold.1
  (43 shorter events, 0.9 us)
Async XLA Ops:
  4.5 7.7 %copy-start.7 = (bf16[8,768]{1,0:T(8,128)(2,1)S(1)}, bf16[8,768]{1,0:T(8,128)(2,1)}, u32[]{:S(2)}) copy-start(bf16[8,768]{1,0:T(8,128)(2,1)} %get-tuple-element.15) | copy-start | bytes 36868
  4.5 9.2 %copy-start.6 = (bf16[8,768]{1,0:T(8,128)(2,1)S(1)}, bf16[8,768]{1,0:T(8,128)(2,1)}, u32[]{:S(2)}) copy-start(bf16[8,768]{1,0:T(8,128)(2,1)} %get-tuple-element.16) | copy-start | bytes 36868
  4.6 11.9 %copy-start.8 = (f32[12]{0:T(128)S(1)}, f32[12]{0:T(128)}, u32[]{:S(2)}) copy-start(f32[12]{0:T(128)} %param.16) | copy-start | bytes 148
  4.6 11.9 %copy-start.5 = (f32[8,768]{1,0:T(8,128)S(1)}, f32[8,768]{1,0:T(8,128)}, u32[]{:S(2)}) copy-start(f32[8,768]{1,0:T(8,128)} %param.17) | copy-start | bytes 73732
  4.6 34.0 %copy-start.4 = (bf16[1,8,8,768]{3,2,1,0:T(8,128)(2,1)S(1)}, bf16[1,8,8,768]{3,2,1,0:T(8,128)(2,1)}, u32[]{:S(2)}) copy-start(bf16[1,8,8,768]{3,2,1,0:T(8,128)(2,1)} %param.12) | copy-start | bytes 294916
  4.6 44.1 %all-to-all-start = ((bf16[16,2,128,256]{3,2,1,0:T(8,128)(2,1)}), bf16[16,2,128,256]{3,2,1,0:T(8,128)(2,1)S(1)}, u32[]{:S(2)}, u32[]{:S(2)}) async-start(bf16[16,2,128,256]{3,2,1,0:T(8,128)(2,1)} %get-tuple-element.14), calls=%async_computation | async-start | bytes 4194304 | tf_op jit(solution)/shard_map/all_to_all | solution.py:484
  12.2 34.5 %copy-start = (bf16[256,768]{1,0:T(8,128)(2,1)S(1)}, bf16[256,768]{1,0:T(8,128)(2,1)}, u32[]{:S(2)}) copy-start(bf16[256,768]{1,0:T(8,128)(2,1)} %outer_ref.3) | copy-start | bytes 1179652
  12.2 34.5 %copy-start.3 = (bf16[1,8,8,768]{3,2,1,0:T(8,128)(2,1)S(1)}, bf16[1,8,8,768]{3,2,1,0:T(8,128)(2,1)}, u32[]{:S(2)}) copy-start(bf16[1,8,8,768]{3,2,1,0:T(8,128)(2,1)} %param.11) | copy-start | bytes 294916
  12.2 26.3 %collective-permute-start = (bf16[8,768]{1,0:T(8,128)(2,1)S(1)}, bf16[8,768]{1,0:T(8,128)(2,1)S(1)}, u32[]{:S(2)}, u32[]{:S(2)}) collective-permute-start(bf16[8,768]{1,0:T(8,128)(2,1)S(1)} %copy-done.7), channel_id=1, source_target_pairs={{0,2},{2,4},{4,6},{6,8},{8,10},{10,12},{12,14},{14,16},{16,18},{18... | collective-permute-start | bytes 36872 | tf_op jit(solution)/shard_map/ppermute | solution.py:31
  13.7 24.8 %collective-permute-start.1 = (bf16[8,768]{1,0:T(8,128)(2,1)S(1)}, bf16[8,768]{1,0:T(8,128)(2,1)S(1)}, u32[]{:S(2)}, u32[]{:S(2)}) collective-permute-start(bf16[8,768]{1,0:T(8,128)(2,1)S(1)} %copy-done.6), channel_id=1, source_target_pairs={{2,0},{4,2},{6,4},{8,6},{10,8},{12,10},{14,12},{16,14},{18,16},{20... | collective-permute-start | bytes 36872 | tf_op jit(solution)/shard_map/ppermute | solution.py:32
  38.6 7.8 %collective-permute-start.2 = (bf16[1,10,768]{2,1,0:T(8,128)(2,1)S(1)}, bf16[1,10,768]{2,1,0:T(8,128)(2,1)S(1)}, u32[]{:S(2)}, u32[]{:S(2)}) collective-permute-start(bf16[1,10,768]{2,1,0:T(8,128)(2,1)S(1)} %get-tuple-element.35), channel_id=1, source_target_pairs={{0,32},{32,64},{64,96},{96,128},{128,160},{160,192},{192,224},{224... | collective-permute-start | bytes 46088 | tf_op jit(solution)/shard_map/ppermute | solution.py:35
  40.6 5.8 %collective-permute-start.3 = (bf16[1,10,768]{2,1,0:T(8,128)(2,1)S(1)}, bf16[1,10,768]{2,1,0:T(8,128)(2,1)S(1)}, u32[]{:S(2)}, u32[]{:S(2)}) collective-permute-start(bf16[1,10,768]{2,1,0:T(8,128)(2,1)S(1)} %get-tuple-element.36), channel_id=1, source_target_pairs={{32,0},{64,32},{96,64},{128,96},{160,128},{192,160},{224,192},{0,2... | collective-permute-start | bytes 46088 | tf_op jit(solution)/shard_map/ppermute | solution.py:38
  44.8 1.9 %copy-start.1 = (bf16[768,768]{1,0:T(8,128)(2,1)S(1)}, bf16[768,768]{1,0:T(8,128)(2,1)}, u32[]{:S(2)}) copy-start(bf16[768,768]{1,0:T(8,128)(2,1)} %probe_ref.1) | copy-start | bytes 3538948
  44.8 3.9 %copy-start.2 = (bf16[256,256]{1,0:T(8,128)(2,1)S(1)}, bf16[256,256]{1,0:T(8,128)(2,1)}, u32[]{:S(2)}) copy-start(bf16[256,256]{1,0:T(8,128)(2,1)} %inner_ref.1) | copy-start | bytes 393220
  59.6 1.6 %collective-permute-start.8 = (bf16[128,1024]{1,0:T(8,128)(2,1)S(1)}, bf16[128,1024]{1,0:T(8,128)(2,1)S(1)}, u32[]{:S(2)}, u32[]{:S(2)}) collective-permute-start(bf16[128,1024]{1,0:T(8,128)(2,1)S(1)} %get-tuple-element.22), channel_id=1, source_target_pairs={{0,1},{1,0},{2,3},{3,2},{4,5},{5,4},{6,7},{7,6},{8,9},{9,8},{10,11... | collective-permute-start | bytes 786440 | tf_op jit(solution)/shard_map/ppermute | solution.py:444
  100.5 15.0 %all-to-all-start.3 = ((bf16[16,8,1024]{2,1,0:T(8,128)(2,1)}), bf16[16,8,1024]{2,1,0:T(8,128)(2,1)S(1)}, u32[]{:S(2)}, u32[]{:S(2)}) async-start(bf16[16,8,1024]{2,1,0:T(8,128)(2,1)} %broadcast_in_dim.35), calls=%async_computation.3 | async-start | bytes 524288 | tf_op jit(solution)/shard_map/all_to_all | solution.py:454
  105.9 6.3 %collective-permute-start.4 = (bf16[8,1,768]{2,1,0:T(2,128)(2,1)S(1)}, bf16[8,1,768]{2,1,0:T(2,128)(2,1)S(1)}, u32[]{:S(2)}, u32[]{:S(2)}) collective-permute-start(bf16[8,1,768]{2,1,0:T(2,128)(2,1)S(1)} %get-tuple-element.37), channel_id=1, source_target_pairs={{0,2},{2,4},{4,6},{6,8},{8,10},{10,12},{12,14},{14,16},{16,18},{18... | collective-permute-start | bytes 36872 | tf_op jit(solution)/shard_map/ppermute | solution.py:35
  107.4 4.7 %collective-permute-start.5 = (bf16[8,1,768]{2,1,0:T(2,128)(2,1)S(1)}, bf16[8,1,768]{2,1,0:T(2,128)(2,1)S(1)}, u32[]{:S(2)}, u32[]{:S(2)}) collective-permute-start(bf16[8,1,768]{2,1,0:T(2,128)(2,1)S(1)} %get-tuple-element.38), channel_id=1, source_target_pairs={{2,0},{4,2},{6,4},{8,6},{10,8},{12,10},{14,12},{16,14},{18,16},{20... | collective-permute-start | bytes 36872 | tf_op jit(solution)/shard_map/ppermute | solution.py:38
  112.2 5.1 %collective-permute-start.6 = (bf16[1,10,768]{2,1,0:T(8,128)(2,1)S(1)}, bf16[1,10,768]{2,1,0:T(8,128)(2,1)S(1)}, u32[]{:S(2)}, u32[]{:S(2)}) collective-permute-start(bf16[1,10,768]{2,1,0:T(8,128)(2,1)S(1)} %get-tuple-element.33), channel_id=1, source_target_pairs={{0,32},{32,64},{64,96},{96,128},{128,160},{160,192},{192,224},{224... | collective-permute-start | bytes 46088 | tf_op jit(solution)/shard_map/ppermute | solution.py:35
  112.8 4.5 %collective-permute-start.7 = (bf16[1,10,768]{2,1,0:T(8,128)(2,1)S(1)}, bf16[1,10,768]{2,1,0:T(8,128)(2,1)S(1)}, u32[]{:S(2)}, u32[]{:S(2)}) collective-permute-start(bf16[1,10,768]{2,1,0:T(8,128)(2,1)S(1)} %get-tuple-element.34), channel_id=1, source_target_pairs={{32,0},{64,32},{96,64},{128,96},{160,128},{192,160},{224,192},{0,2... | collective-permute-start | bytes 46088 | tf_op jit(solution)/shard_map/ppermute | solution.py:38
  115.5 2.7 %collective-permute-start.9 = (bf16[128,1024]{1,0:T(8,128)(2,1)S(1)}, bf16[128,1024]{1,0:T(8,128)(2,1)S(1)}, u32[]{:S(2)}, u32[]{:S(2)}) collective-permute-start(bf16[128,1024]{1,0:T(8,128)(2,1)S(1)} %bitcast.15), channel_id=1, source_target_pairs={{0,1},{1,0},{2,3},{3,2},{4,5},{5,4},{6,7},{7,6},{8,9},{9,8},{10,11... | collective-permute-start | bytes 786440 | tf_op jit(solution)/shard_map/ppermute | solution.py:457
